TPU v7x, 256 devices: a whole 4x4x8 slice. The times are simulated.
256 devices in a mesh: view: 32 (over z, y), head: 8 (over x, core).
Axes of the slice: x: 4, y: 4, z: 8, core: 2. Of those that a mesh axis runs over, the one named last changes fastest.
Arguments:
- query_rows: bfloat16 [32768, 1024], P('view', 'head'), may hold values from -20 to 20
- key_rows: bfloat16 [32768, 1024], P('view', 'head'), may hold values from -6 to 6
- value_rows: bfloat16 [32768, 1024], P('view', 'head'), may hold values from -12 to 12
- out_weight: bfloat16 [1024, 1024], replicated, may hold values from -0.1875 to 0.1875
- out_grad: bfloat16 [32768, 1024], P('view', 'head'), may hold values from -12 to 12
- source_view: int32 [32, 16], replicated, may hold values from 0 to 31, as said below
- source_block: int32 [32, 16], replicated, may hold values from 0 to 7
Outputs:
- mixed_out: bfloat16 [32768, 1024], P('view', 'head')
- query_grad: bfloat16 [32768, 1024], P('view', 'head')
- key_grad: bfloat16 [32768, 1024], P('view', 'head')
- value_grad: bfloat16 [32768, 1024], P('view', 'head')
Inputs may be any that keep to these rules, and one draw needn't show every extreme that they name: `source_view`: for each query view the 16 slots name distinct pairs of source view and block. No source view is named by more than 1 slots of one query view, and for every query view some source view is named by exactly 1 of its slots.
All inputs are finite; a program needn't handle non-finite values.
Results may differ from a plain program's by a relative error of at most 0.014.
Values may be sent and summed in bfloat16 or wider, within the bound.
A program may use at most 128 MiB of HBM per device.

v0:
```python
import jax
import jax.numpy as jnp
from jax import lax
from jax.sharding import PartitionSpec as P

HEAD_DIM = 64
BLOCK_TOKENS = 128


def cut_along(value, dim, length):
    shape = value.shape
    pieces = value.reshape(*shape[:dim], length, shape[dim] // length, *shape[dim + 1 :])
    return jnp.moveaxis(pieces, dim, 0)


def summed_on_arrival(value, axis, dim):
    pieces = cut_along(value, dim, lax.axis_size(axis))
    arrived = lax.all_to_all(pieces, axis, split_axis=0, concat_axis=0, tiled=True)
    return arrived.astype(jnp.float32).sum(axis=0)


def from_everyone(value, axis):
    length = lax.axis_size(axis)
    return lax.all_to_all(
        jnp.broadcast_to(value[None], (length, *value.shape)), axis, 0, 0, tiled=True
    )


def joined_along(pieces, dim):
    shape = list(pieces.shape[1:])
    shape[dim] *= pieces.shape[0]
    return jnp.moveaxis(pieces, 0, dim).reshape(shape)


def collect(value, axis, dim):
    pieces = from_everyone(value, axis)
    return joined_along(pieces, dim)


def score_rows(query_part, key_heads, score_scale):
    return (
        jnp.einsum("qhd,khd->hqk", query_part, key_heads, preferred_element_type=jnp.float32)
        * score_scale
    )


def body(query_rows, key_rows, value_rows, out_weight, out_grad, source_view, source_block):
    tokens = query_rows.shape[0]
    columns = query_rows.shape[1]
    heads_here = columns // HEAD_DIM
    slot_count = source_view.shape[1]
    key_count = slot_count * BLOCK_TOKENS
    peer_count = lax.axis_size("view")
    capacity = max(1, 2 * slot_count // peer_count)
    block_count = tokens // BLOCK_TOKENS
    view_index = lax.axis_index("view")
    head_index = lax.axis_index("head")
    score_scale = HEAD_DIM ** (-0.5)
    slot_order = jnp.arange(slot_count, dtype=jnp.int32)
    same_view = source_view[:, :, None] == source_view[:, None, :]
    earlier = slot_order[None, :] < slot_order[:, None]
    slot_rank = jnp.sum((same_view & earlier[None]).astype(jnp.int32), axis=2)
    copy_order = jnp.arange(capacity, dtype=jnp.int32)
    matched = (source_view == view_index)[:, :, None] & (
        slot_rank[:, :, None] == copy_order[None, None, :]
    )
    filled = jnp.any(matched, axis=1)
    chosen = jnp.sum(jnp.where(matched, source_block[:, :, None], 0), axis=1)
    own_view = lax.dynamic_index_in_dim(source_view, view_index, 0, keepdims=False)
    own_rank = lax.dynamic_index_in_dim(slot_rank, view_index, 0, keepdims=False)
    landing = own_view * capacity + own_rank
    joined = jnp.concatenate([key_rows, value_rows], axis=1)
    outgoing = jnp.take(
        joined.reshape(block_count, BLOCK_TOKENS, 2 * columns), chosen.reshape(-1), axis=0
    )
    outgoing = outgoing.reshape(peer_count, capacity, BLOCK_TOKENS, 2 * columns)
    incoming = lax.all_to_all(outgoing, "view", split_axis=0, concat_axis=0, tiled=True)
    fetched = jnp.take(
        incoming.reshape(peer_count * capacity, BLOCK_TOKENS, 2 * columns), landing, axis=0
    )
    fetched = fetched.reshape(key_count, 2 * columns)
    query_block = min(512, tokens)
    block_total = tokens // query_block
    key_heads = fetched[:, :columns].reshape(key_count, heads_here, HEAD_DIM)
    value_heads = fetched[:, columns:].reshape(key_count, heads_here, HEAD_DIM)
    query_heads = query_rows.reshape(block_total, query_block, heads_here, HEAD_DIM)

    def forward_step(query_part):
        scores = score_rows(query_part, key_heads, score_scale)
        row_top = jnp.max(scores, axis=-1, keepdims=True)
        shifted = jnp.exp(scores - row_top)
        row_total = jnp.sum(shifted, axis=-1, keepdims=True)
        weights = (shifted / row_total).astype(jnp.bfloat16)
        out_part = jnp.einsum(
            "hqk,khd->qhd", weights, value_heads, preferred_element_type=jnp.float32
        )
        return (out_part.astype(jnp.bfloat16), row_top, row_total)

    attended, row_tops, row_totals = lax.map(forward_step, query_heads)
    attended_rows = attended.reshape(tokens, columns)
    own_rows = lax.dynamic_slice_in_dim(out_weight, head_index * columns, columns, 0)
    part_weight = own_rows
    summed_rows = summed_on_arrival(
        lax.dot_general(
            part_weight, attended_rows, (((0,), (1,)), ((), ())), preferred_element_type=jnp.float32
        ).astype(jnp.bfloat16),
        "head",
        0,
    )
    mixed_out = summed_rows.T.astype(jnp.bfloat16)
    part_weight = own_rows
    attended_grad = lax.dot_general(
        collect(out_grad, "head", 1),
        part_weight,
        (((1,), (1,)), ((), ())),
        preferred_element_type=jnp.float32,
    )
    grad_heads = attended_grad.astype(jnp.bfloat16).reshape(
        block_total, query_block, heads_here, HEAD_DIM
    )

    def backward_step(totals, inputs):
        key_total, value_total = totals
        query_part, out_part, grad_part, row_top, row_total = inputs
        scores = score_rows(query_part, key_heads, score_scale)
        probability = jnp.exp(scores - row_top) / row_total
        weights = probability.astype(jnp.bfloat16)
        grad_prob = jnp.einsum(
            "qhd,khd->hqk", grad_part, value_heads, preferred_element_type=jnp.float32
        )
        row_delta = jnp.einsum(
            "qhd,qhd->hq", out_part, grad_part, preferred_element_type=jnp.float32
        )[:, :, None]
        grad_scores = (probability * (grad_prob - row_delta)).astype(jnp.bfloat16)
        query_part_grad = (
            jnp.einsum("hqk,khd->qhd", grad_scores, key_heads, preferred_element_type=jnp.float32)
            * score_scale
        )
        key_total = (
            key_total
            + jnp.einsum(
                "hqk,qhd->khd", grad_scores, query_part, preferred_element_type=jnp.float32
            )
            * score_scale
        )
        value_total = value_total + jnp.einsum(
            "hqk,qhd->khd", weights, grad_part, preferred_element_type=jnp.float32
        )
        return ((key_total, value_total), query_part_grad.astype(jnp.bfloat16))

    zero_keys = jnp.zeros((key_count, heads_here, HEAD_DIM), jnp.float32)
    (key_total, value_total), query_grads = lax.scan(
        backward_step,
        (zero_keys, zero_keys),
        (query_heads, attended, grad_heads, row_tops, row_totals),
    )
    query_grad = query_grads.reshape(tokens, columns)
    slot_grads = jnp.concatenate(
        [key_total.reshape(key_count, columns), value_total.reshape(key_count, columns)], axis=1
    )
    slot_grads = slot_grads.reshape(slot_count, BLOCK_TOKENS * 2 * columns)
    placing = (
        landing[None, :] == jnp.arange(peer_count * capacity, dtype=jnp.int32)[:, None]
    ).astype(jnp.float32)
    outgoing_grads = jnp.dot(placing, slot_grads, precision=lax.Precision.HIGHEST).reshape(
        peer_count, capacity, BLOCK_TOKENS, 2 * columns
    )
    returned = lax.all_to_all(
        outgoing_grads.astype(jnp.bfloat16), "view", split_axis=0, concat_axis=0, tiled=True
    ).astype(outgoing_grads.dtype)
    gathering = (
        chosen.reshape(-1)[None, :] == jnp.arange(block_count, dtype=jnp.int32)[:, None]
    ) & filled.reshape(-1)[None, :]
    summed = jnp.dot(
        gathering.astype(jnp.float32),
        returned.reshape(peer_count * capacity, BLOCK_TOKENS * 2 * columns),
        precision=lax.Precision.HIGHEST,
    )
    summed = summed.reshape(tokens, 2 * columns)
    key_grad = summed[:, :columns].astype(jnp.bfloat16)
    value_grad = summed[:, columns:].astype(jnp.bfloat16)
    return (mixed_out, query_grad, key_grad, value_grad)


def solution(mesh):
    placed = (
        P("view", "head"),
        P("view", "head"),
        P("view", "head"),
        P(),
        P("view", "head"),
        P(),
        P(),
    )
    return jax.shard_map(
        body,
        mesh=mesh,
        in_specs=placed,
        out_specs=(P("view", "head"), P("view", "head"), P("view", "head"), P("view", "head")),
        check_vma=False,
    )
```

profile of v0, /device:TPU:2, one launch (start us, length us, event | category | flops | bytes accessed | tf_op | source)
XLA Modules:
  0.0 223.8 jit_solution(751368551320462493)
XLA Ops:
  0.7 1.2 copy.56
  1.9 1.6 broadcast_in_dim.70
  3.5 6.5 %all-to-all-start.2 = ((bf16[8,1024,128]{1,2,0:T(8,128)(2,1)}), bf16[8,1024,128]{1,2,0:T(8,128)(2,1)}, u32[]{:S(2)}, u32[]{:S(2)}) async-start(bf16[8,1024,128]{1,2,0:T(8,128)(2,1)} %broadcast_in_dim.70), calls=%async_computation.2 | async-start | bytes 4194304 | tf_op jit(solution)/shard_map/all_to_all | solution.py:24
  10.8 2.0 gather_fusion
  12.9 3.2 %bitcast_select_fusion = bf16[32,1,128,256]{3,2,1,0:T(8,128)(2,1)} fusion(bf16[32,128,256]{2,1,0:T(8,128)(2,1)} %gather_fusion, pred[32]{0:T(512)(128)(4,1)S(1)} %compare_and_fusion.1), kind=kLoop, calls=%fused_computation.52 | loop fusion | flops 1048576 | bytes 4194336 | tf_op jit(solution)/shard_map/jit(_take)/select_n | solution.py:73
  16.1 19.7 %all-to-all-done.2 = bf16[8,1024,128]{1,2,0:T(8,128)(2,1)} async-done(((bf16[8,1024,128]{1,2,0:T(8,128)(2,1)}), bf16[8,1024,128]{1,2,0:T(8,128)(2,1)}, u32[]{:S(2)}, u32[]{:S(2)}) %all-to-all-start.2) | async-done | bytes 2097184 | tf_op jit(solution)/shard_map/all_to_all | solution.py:24
  35.8 9.9 %all-to-all-start = ((bf16[32,1,128,256]{3,2,1,0:T(8,128)(2,1)}), bf16[32,1,128,256]{3,2,1,0:T(8,128)(2,1)}, u32[]{:S(2)}, u32[]{:S(2)}) async-start(bf16[32,1,128,256]{3,2,1,0:T(8,128)(2,1)} %bitcast_select_fusion), calls=%async_computation | async-start | bytes 4194304 | tf_op jit(solution)/shard_map/all_to_all | solution.py:77
  45.9 1.1 reshape.191
  46.9 1.3 copy.54
  49.0 2.7 %fusion.40 = bf16[1024,128]{0,1:T(8,128)(2,1)} fusion(bf16[1024,1024]{0,1:T(8,128)(2,1)} %bitcast.20, bf16[1024,1024]{1,0:T(8,128)(2,1)S(1)} %copy-done, s32[]{:T(128)S(6)} %select_n.61), kind=kOutput, calls=%fused_computation.56 | convolution fusion | flops 268566528 | bytes 2621444 | tf_op jit(solution)/shard_map/dot_general | solution.py:112
  51.8 1.9 reshape.162
  53.6 1.7 copy.58
  55.3 40.3 %all-to-all-done = bf16[32,1,128,256]{3,2,1,0:T(8,128)(2,1)} async-done(((bf16[32,1,128,256]{3,2,1,0:T(8,128)(2,1)}), bf16[32,1,128,256]{3,2,1,0:T(8,128)(2,1)}, u32[]{:S(2)}, u32[]{:S(2)}) %all-to-all-start) | async-done | bytes 2097184 | tf_op jit(solution)/shard_map/all_to_all | solution.py:77
  95.6 3.2 %gather_fusion.1 = bf16[16,128,256]{2,1,0:T(8,128)(2,1)} fusion(bf16[32,128,256]{2,1,0:T(8,128)(2,1)} %bitcast.12, s32[1024]{0:T(1024)S(1)} %pad_clamp_fusion), kind=kCustom, calls=%fused_computation.1 | custom fusion | bytes 2097216 | tf_op jit(solution)/shard_map/jit(_take)/gather | solution.py:78
  98.8 1.5 bitcast_select_fusion.1
  100.3 1.1 fusion.55
  101.4 2.1 copy.53
  103.4 2.1 copy.52
  106.2 14.2 %while.29 = (s32[]{:T(128)}, bf16[2,512,2,64]{1,3,2,0:T(8,128)(2,1)}, f32[2,2,512,1]{2,1,3,0:T(2,128)S(1)}, f32[2,2,512,1]{2,1,3,0:T(2,128)S(1)}, bf16[2,512,2,6...) while((s32[]{:T(128)}, ...), condition=%wide.region_5.6_spmd, body=%wide.region_2.5_spmd.sunk | while | flops 555808768 | bytes 30707900 | solution.py:99
  106.2 2.4 %multiply_reduce_fusion.4 = (f32[2,512]{1,0:T(2,128)S(1)}, f32[2,512,2048]{2,1,0:T(8,128)S(1)}) fusion(bf16[2048,2,64]{0,2,1:T(8,128)(2,1)} %get-tuple-element.412, bf16[2,512,2,64]{1,3,2,0:T(8,128)(2,1)S(1)} %get-tuple-element.411, s32[]{:T(128)S(6)} %copy.99), kind=kOutput, calls=%fused_computation.4.clone.1 | convolution fusion | flops 272628736 | bytes 9048068 | tf_op jit(solution)/shard_map/while/body/eval_jaxpr/qhd,khd->hqk/dot_general | solution.py:42
  108.7 1.6 fusion.86
  110.3 2.3 %fusion.87 = bf16[2,512,2,64]{1,3,2,0:T(8,128)(2,1)S(1)} fusion(bf16[2,512,2,64]{1,3,2,0:T(8,128)(2,1)S(1)} %copy-done.9, s32[]{:T(128)S(6)} %copy.99, bf16[2048,2,64]{0,2,1:T(8,128)(2,1)S(1)} %copy-done.5, f32[2,512,2048]{2,1,0:T(8,128)S(1)} %get-tuple-element.374, f32[2,512]{1,0:T(2,128)S(1)} %fusion.86, f32[2,512]{1,0:T(2,128)S(1)} %get-tuple-element.375), kind=kOutput, calls=%fused_computation.9.clone.1 | convolution fusion | flops 276889600 | bytes 9052164 | tf_op jit(solution)/shard_map/while/body/eval_jaxpr/hqk,khd->qhd/dot_general | solution.py:94
  113.3 2.4 %multiply_reduce_fusion.4 = (f32[2,512]{1,0:T(2,128)S(1)}, f32[2,512,2048]{2,1,0:T(8,128)S(1)}) fusion(bf16[2048,2,64]{0,2,1:T(8,128)(2,1)} %get-tuple-element.412, bf16[2,512,2,64]{1,3,2,0:T(8,128)(2,1)S(1)} %get-tuple-element.411, s32[]{:T(128)S(6)} %copy.99), kind=kOutput, calls=%fused_computation.4.clone.1 | convolution fusion | flops 272628736 | bytes 9048068 | tf_op jit(solution)/shard_map/while/body/eval_jaxpr/qhd,khd->hqk/dot_general | solution.py:42
  115.8 1.6 fusion.86
  117.4 2.3 %fusion.87 = bf16[2,512,2,64]{1,3,2,0:T(8,128)(2,1)S(1)} fusion(bf16[2,512,2,64]{1,3,2,0:T(8,128)(2,1)S(1)} %copy-done.9, s32[]{:T(128)S(6)} %copy.99, bf16[2048,2,64]{0,2,1:T(8,128)(2,1)S(1)} %copy-done.5, f32[2,512,2048]{2,1,0:T(8,128)S(1)} %get-tuple-element.374, f32[2,512]{1,0:T(2,128)S(1)} %fusion.86, f32[2,512]{1,0:T(2,128)S(1)} %get-tuple-element.375), kind=kOutput, calls=%fused_computation.9.clone.1 | convolution fusion | flops 276889600 | bytes 9052164 | tf_op jit(solution)/shard_map/while/body/eval_jaxpr/hqk,khd->qhd/dot_general | solution.py:94
  120.4 1.2 copy.55
  121.7 2.1 convolution_convert_fusion.1
  123.8 5.8 %all-to-all-start.1 = ((bf16[8,128,1024]{2,1,0:T(8,128)(2,1)}), bf16[8,128,1024]{2,1,0:T(8,128)(2,1)}, u32[]{:S(2)}, u32[]{:S(2)}) async-start(bf16[8,128,1024]{2,1,0:T(8,128)(2,1)} %bitcast.154), calls=%async_computation.1 | async-start | bytes 4194304 | tf_op jit(solution)/shard_map/all_to_all | solution.py:18
  130.3 21.9 %while.30 = (s32[]{:T(128)}, f32[2048,2,64]{0,2,1:T(8,128)S(1)}, f32[2048,2,64]{0,2,1:T(8,128)S(1)}, bf16[2,512,2,64]{1,3,2,0:T(8,128)(2,1)}, bf16[2,512,2,64]{1...) while((s32[]{:T(128)}, f32[2048,2,64]{0,2,1:T(8,128)S(1)}, ...), condition=%wide.region_8.9_spmd.clone, body=%wide.region_7.8_spmd.clone.sunk | while | flops 1358560256 | bytes 53379412 | solution.py:152
  133.4 2.9 %exponential_divide_fusion.2 = f32[2,512,2048]{2,1,0:T(8,128)S(1)} fusion(bf16[2048,2,64]{0,2,1:T(8,128)(2,1)S(1)} %get-tuple-element.446, f32[2,512]{1,0:T(2,128)S(1)} %get-tuple-element.389, f32[2,512]{1,0:T(2,128)S(1)} %get-tuple-element.390, bf16[2,512,2,64]{1,3,2,0:T(8,128)(2,1)} %copy-done.7, s32[]{:T(128)S(6)} %copy.111), kind=kOutput, calls=%fused_computation.18.clone.1 | convolution fusion | flops 274726912 | bytes 9052164 | tf_op jit(solution)/shard_map/while/body/eval_jaxpr/qhd,khd->hqk/dot_general | solution.py:42
  136.4 1.0 fusion.99
  137.4 1.4 multiply_convert_fusion.2
  138.8 1.4 fusion.100
  140.2 1.0 fusion.98
  144.4 2.9 %exponential_divide_fusion.2 = f32[2,512,2048]{2,1,0:T(8,128)S(1)} fusion(bf16[2048,2,64]{0,2,1:T(8,128)(2,1)S(1)} %get-tuple-element.446, f32[2,512]{1,0:T(2,128)S(1)} %get-tuple-element.389, f32[2,512]{1,0:T(2,128)S(1)} %get-tuple-element.390, bf16[2,512,2,64]{1,3,2,0:T(8,128)(2,1)} %copy-done.7, s32[]{:T(128)S(6)} %copy.111), kind=kOutput, calls=%fused_computation.18.clone.1 | convolution fusion | flops 274726912 | bytes 9052164 | tf_op jit(solution)/shard_map/while/body/eval_jaxpr/qhd,khd->hqk/dot_general | solution.py:42
  147.3 1.0 fusion.99
  148.3 1.4 multiply_convert_fusion.2
  149.8 1.4 fusion.100
  151.2 1.0 fusion.98
  152.2 1.3 copy.61
  153.8 1.4 pad_maximum_fusion
  155.2 1.6 reshape.166
  156.8 3.5 %convert_bitcast_fusion = bf16[32,1,128,256]{3,0,2,1:T(8,128)(2,1)S(1)} fusion(f32[2,128,8,256]{3,2,1,0:T(8,128)} %bitcast.156, s32[16]{0:T(128)S(1)} %copy-done.21), kind=kOutput, calls=%fused_computation.53 | convolution fusion | flops 202375680 | bytes 4194368 | tf_op jit(solution)/shard_map/dot_general | solution.py:165
  160.3 2.5 %copy.64 = bf16[32,1,128,256]{3,2,1,0:T(8,128)(2,1)} copy(bf16[32,1,128,256]{3,0,2,1:T(8,128)(2,1)S(1)} %convert_bitcast_fusion) | data formatting | bytes 4194304 | tf_op jit(solution)/shard_map/convert_element_type | solution.py:169
  162.8 6.3 %all-to-all-start.3 = ((bf16[32,1,128,256]{3,2,1,0:T(8,128)(2,1)}), bf16[32,1,128,256]{3,2,1,0:T(8,128)(2,1)}, u32[]{:S(2)}, u32[]{:S(2)}) async-start(bf16[32,1,128,256]{3,2,1,0:T(8,128)(2,1)} %copy.64), calls=%async_computation.3 | async-start | bytes 4194304 | tf_op jit(solution)/shard_map/all_to_all | solution.py:168
  170.5 2.0 reduce_sum.44
  173.3 46.0 %all-to-all-done.3 = bf16[32,1,128,256]{3,2,1,0:T(8,128)(2,1)} async-done(((bf16[32,1,128,256]{3,2,1,0:T(8,128)(2,1)}), bf16[32,1,128,256]{3,2,1,0:T(8,128)(2,1)}, u32[]{:S(2)}, u32[]{:S(2)}) %all-to-all-start.3) | async-done | bytes 2097184 | tf_op jit(solution)/shard_map/all_to_all | solution.py:168
  219.3 2.9 %copy.80 = bf16[4,8,128,256]{3,1,2,0:T(8,128)(2,1)S(1)} copy(bf16[4,8,128,256]{3,2,1,0:T(8,128)(2,1)} %bitcast.51) | data formatting | bytes 4194304
  (108 shorter events, 14.8 us)
Async XLA Ops:
  0.6 48.4 %copy-start = (bf16[1024,1024]{1,0:T(8,128)(2,1)S(1)}, bf16[1024,1024]{1,0:T(8,128)(2,1)}, u32[]{:S(2)}) copy-start(bf16[1024,1024]{1,0:T(8,128)(2,1)} %param.14) | copy-start | bytes 6291460
  0.6 9.4 %copy-start.17 = (s32[32,16]{0,1:T(8,128)S(1)}, s32[32,16]{0,1:T(8,128)}, u32[]{:S(2)}) copy-start(s32[32,16]{0,1:T(8,128)} %param.16) | copy-start | bytes 6148
  0.7 10.0 %copy-start.18 = (s32[32,16]{0,1:T(8,128)S(1)}, s32[32,16]{0,1:T(8,128)}, u32[]{:S(2)}) copy-start(s32[32,16]{0,1:T(8,128)} %param.17) | copy-start | bytes 6148
  0.7 10.0 %copy-start.15 = (bf16[1024,128]{1,0:T(8,128)(2,1)S(1)}, bf16[1024,128]{1,0:T(8,128)(2,1)}, u32[]{:S(2)}) copy-start(bf16[1024,128]{1,0:T(8,128)(2,1)} %param.13) | copy-start | bytes 786436
  0.7 10.0 %copy-start.16 = (bf16[1024,128]{1,0:T(8,128)(2,1)S(1)}, bf16[1024,128]{1,0:T(8,128)(2,1)}, u32[]{:S(2)}) copy-start(bf16[1024,128]{1,0:T(8,128)(2,1)} %param.12) | copy-start | bytes 786436
  3.5 32.3 %all-to-all-start.2 = ((bf16[8,1024,128]{1,2,0:T(8,128)(2,1)}), bf16[8,1024,128]{1,2,0:T(8,128)(2,1)}, u32[]{:S(2)}, u32[]{:S(2)}) async-start(bf16[8,1024,128]{1,2,0:T(8,128)(2,1)} %broadcast_in_dim.70), calls=%async_computation.2 | async-start | bytes 4194304 | tf_op jit(solution)/shard_map/all_to_all | solution.py:24
  10.7 2.2 copy-start.22
  12.8 33.0 %copy-start.14 = (bf16[1024,128]{1,0:T(8,128)(2,1)S(1)}, bf16[1024,128]{1,0:T(8,128)(2,1)}, u32[]{:S(2)}) copy-start(bf16[1024,128]{1,0:T(8,128)(2,1)} %param.11) | copy-start | bytes 786436
  35.8 59.8 %all-to-all-start = ((bf16[32,1,128,256]{3,2,1,0:T(8,128)(2,1)}), bf16[32,1,128,256]{3,2,1,0:T(8,128)(2,1)}, u32[]{:S(2)}, u32[]{:S(2)}) async-start(bf16[32,1,128,256]{3,2,1,0:T(8,128)(2,1)} %bitcast_select_fusion), calls=%async_computation | async-start | bytes 4194304 | tf_op jit(solution)/shard_map/all_to_all | solution.py:77
  48.4 0.6 copy-start.20
  108.7 1.7 copy-start.5
  108.7 1.7 copy-start.9
  112.6 0.7 copy-start.10
  115.7 1.7 copy-start.5
  115.7 1.7 copy-start.9
  119.7 0.7 copy-start.10
  123.7 6.5 %copy-start.2 = (bf16[2048,2,64]{0,2,1:T(8,128)(2,1)S(1)}, bf16[2048,2,64]{0,2,1:T(8,128)(2,1)}, u32[]{:S(2)}) copy-start(bf16[2048,2,64]{0,2,1:T(8,128)(2,1)} %get-tuple-element.454) | copy-start | bytes 1572868
  123.8 6.5 %copy-start.3 = (f32[2048,2,64]{0,2,1:T(8,128)S(1)}, f32[2048,2,64]{0,2,1:T(8,128)}, u32[]{:S(2)}) copy-start(f32[2048,2,64]{0,2,1:T(8,128)} %custom-call.1) | copy-start | bytes 3145732
  123.8 39.1 %all-to-all-start.1 = ((bf16[8,128,1024]{2,1,0:T(8,128)(2,1)}), bf16[8,128,1024]{2,1,0:T(8,128)(2,1)}, u32[]{:S(2)}, u32[]{:S(2)}) async-start(bf16[8,128,1024]{2,1,0:T(8,128)(2,1)} %bitcast.154), calls=%async_computation.1 | async-start | bytes 4194304 | tf_op jit(solution)/shard_map/all_to_all | solution.py:18
  130.3 0.7 copy-start.7
  133.4 2.9 %copy-start.4 = (bf16[2,512,2,64]{1,3,2,0:T(8,128)(2,1)S(1)}, bf16[2,512,2,64]{1,3,2,0:T(8,128)(2,1)}, u32[]{:S(2)}) copy-start(bf16[2,512,2,64]{1,3,2,0:T(8,128)(2,1)} %get-tuple-element.449) | copy-start | bytes 786436 | tf_op jit(solution)/shard_map/while
  136.3 1.0 copy-start.6
  137.4 1.4 copy-start.11
  138.8 1.4 copy-start.8
  140.2 1.0 copy-start.12
  141.2 0.7 copy-start.7
  144.4 2.9 %copy-start.4 = (bf16[2,512,2,64]{1,3,2,0:T(8,128)(2,1)S(1)}, bf16[2,512,2,64]{1,3,2,0:T(8,128)(2,1)}, u32[]{:S(2)}) copy-start(bf16[2,512,2,64]{1,3,2,0:T(8,128)(2,1)} %get-tuple-element.449) | copy-start | bytes 786436 | tf_op jit(solution)/shard_map/while
  147.3 1.0 copy-start.6
  148.3 1.4 copy-start.11
  149.8 1.4 copy-start.8
  151.2 1.0 copy-start.12
  153.8 2.9 %copy-start.21 = (s32[16]{0:T(128)S(1)}, s32[16]{0:T(128)}, u32[]{:S(2)}) copy-start(s32[16]{0:T(128)} %copy-done.20) | copy-start | bytes 196
  160.3 8.9 %copy-start.13 = (bf16[2,512,2,64]{1,3,2,0:T(8,128)(2,1)S(1)}, bf16[2,512,2,64]{1,3,2,0:T(8,128)(2,1)}, u32[]{:S(2)}) copy-start(bf16[2,512,2,64]{1,3,2,0:T(8,128)(2,1)} %get-tuple-element.105) | copy-start | bytes 786436
  162.8 56.5 %all-to-all-start.3 = ((bf16[32,1,128,256]{3,2,1,0:T(8,128)(2,1)}), bf16[32,1,128,256]{3,2,1,0:T(8,128)(2,1)}, u32[]{:S(2)}, u32[]{:S(2)}) async-start(bf16[32,1,128,256]{3,2,1,0:T(8,128)(2,1)} %copy.64), calls=%async_computation.3 | async-start | bytes 4194304 | tf_op jit(solution)/shard_map/all_to_all | solution.py:168
  169.2 53.1 %copy-start.19 = (pred[32]{0:T(512)(128)(4,1)S(1)}, pred[32]{0:T(512)(128)(4,1)}, u32[]{:S(2)}) copy-start(pred[32]{0:T(512)(128)(4,1)} %get-tuple-element.257) | copy-start | bytes 100
  169.2 53.1 %copy-start.23 = (s32[32]{0:T(128)S(1)}, s32[32]{0:T(128)}, u32[]{:S(2)}) copy-start(s32[32]{0:T(128)} %copy-done.22) | copy-start | bytes 388
  219.3 4.4 %copy-start.1 = (bf16[1024,1024]{1,0:T(8,128)(2,1)S(1)}, bf16[1024,1024]{1,0:T(8,128)(2,1)}, u32[]{:S(2)}) copy-start(bf16[1024,1024]{1,0:T(8,128)(2,1)} %param.14) | copy-start | bytes 6291460
where the time goes:
time: 225 us; the launch traced here: 224 us
  waiting for transfers between devices  106 us (47%)
  local copies, waits for them, and re-layouts  39.9 us (18%)
  matrix products  33.4 us (15%)
  starting transfers between devices  28.5 us (13%)
  other arithmetic  14.6 us (6%)
    all_to_all x1, waiting for transfers between devices, body(): lax.all_to_all(outgoing_grads.astype(jnp.bfloat16), 'view', split_axis=0,...  46 us
    all_to_all x1, waiting for transfers between devices, body(): lax.all_to_all(outgoing, 'view', split_axis=0, concat_axis=0, tiled=True)  40.3 us
    all_to_all x1, waiting for transfers between devices, from_everyone(): lax.all_to_all(jnp.broadcast_to(value[None], (length, *value.shape)), axi...  19.7 us
    dot_general x4, matrix products, score_rows(): jnp.einsum('qhd,khd->hqk', query_part, key_heads, preferred_element_type=...  10.6 us
    all_to_all x1, starting transfers between devices, body(): lax.all_to_all(outgoing, 'view', split_axis=0, concat_axis=0, tiled=True)  9.95 us
    unnamed x37, local copies, waits for them, and re-layouts  8.67 us
    all_to_all x1, starting transfers between devices, from_everyone(): lax.all_to_all(jnp.broadcast_to(value[None], (length, *value.shape)), axi...  6.46 us
    all_to_all x1, starting transfers between devices, body(): lax.all_to_all(outgoing_grads.astype(jnp.bfloat16), 'view', split_axis=0,...  6.29 us
  transfers between devices with their start and end apart: 4, of which 3 were waited for; matrix products, arithmetic and copies ran while one was open for 23% of the time, Pallas kernels for 0%

commit v1 on v0

v1 whole, which is shorter than its diff:
```python
import functools

import jax
import jax.numpy as jnp
from jax import lax
from jax.experimental import pallas as pl
from jax.experimental.pallas import tpu as pltpu
from jax.sharding import PartitionSpec as P

HEAD_DIM = 64
BLOCK = 128
SCALE = HEAD_DIM ** -0.5
LOG2E = 1.4426950408889634
QB = 256
KC = 256


def dot(a, b):
    return jnp.dot(a, b, preferred_element_type=jnp.float32)


def attention_kernel(
    idx, q_ref, rk_ref, rv_ref, da_ref,
    att_ref, dq_ref, dk_ref, dv_ref,
    k_s, v_s, kt_s, vt_s, s_s, p_s, dk_a, dv_a,
):
    slots = idx.shape[0]
    keys = slots * BLOCK
    tokens = q_ref.shape[0]
    for j in range(slots):
        rows = pl.ds(j * BLOCK, BLOCK)
        kb = rk_ref[idx[j]]
        vb = rv_ref[idx[j]]
        k_s[rows, :] = kb
        v_s[rows, :] = vb
        kt_s[:, rows] = kb.T
        vt_s[:, rows] = vb.T
    dk_a[...] = jnp.zeros_like(dk_a)
    dv_a[...] = jnp.zeros_like(dv_a)
    chunks = keys // KC
    lane = lax.broadcasted_iota(jnp.int32, (QB, 2 * HEAD_DIM), 1)

    def step(i, carry):
        qrows = pl.ds(pl.multiple_of(i * QB, QB), QB)
        q = q_ref[qrows, :]
        da = da_ref[qrows, :]
        qt = q.T
        dat = da.T
        atts = []
        dqs = []
        for h in range(2):
            hd = slice(h * HEAD_DIM, (h + 1) * HEAD_DIM)
            mine = (lane // HEAD_DIM) == h
            qh = jnp.where(mine, q, jnp.zeros_like(q))
            dah = jnp.where(mine, da, jnp.zeros_like(da))
            qth = qt[hd, :]
            dath = dat[hd, :]
            top = None
            for c in range(chunks):
                rows = pl.ds(c * KC, KC)
                s = dot(k_s[rows, hd], qth)
                s_s[rows, :] = s
                m = jnp.max(s, axis=0, keepdims=True)
                top = m if top is None else jnp.maximum(top, m)
            shift = top * (SCALE * LOG2E)
            total = jnp.zeros((1, QB), jnp.float32)
            for c in range(chunks):
                rows = pl.ds(c * KC, KC)
                e = jnp.exp2(s_s[rows, :] * (SCALE * LOG2E) - shift)
                s_s[rows, :] = e
                total = total + jnp.sum(e, axis=0, keepdims=True)
            inv = 1.0 / total
            for c in range(chunks):
                rows = pl.ds(c * KC, KC)
                p = s_s[rows, :] * inv
                pb = p.astype(jnp.bfloat16)
                p_s[rows, :] = pb
                dv_a[rows, :] += dot(pb, dah)
            att = dot(vt_s[hd, :], p_s[...]).astype(jnp.bfloat16)
            atts.append(att)
            delta = jnp.sum(
                att.astype(jnp.float32) * dath.astype(jnp.float32), axis=0, keepdims=True
            )
            for c in range(chunks):
                rows = pl.ds(c * KC, KC)
                dp = dot(v_s[rows, hd], dath)
                ds = ((s_s[rows, :] * inv) * (dp - delta)).astype(jnp.bfloat16)
                p_s[rows, :] = ds
                dk_a[rows, :] += dot(ds, qh)
            dqs.append(dot(kt_s[hd, :], p_s[...]) * SCALE)
        att_ref[qrows, :] = jnp.concatenate(atts, axis=0).T
        dq_ref[qrows, :] = jnp.concatenate(dqs, axis=0).astype(jnp.bfloat16).T
        return carry

    lax.fori_loop(0, tokens // QB, step, 0)
    for j in range(slots):
        rows = pl.ds(j * BLOCK, BLOCK)
        dk_ref[idx[j]] = (dk_a[rows, :] * SCALE).astype(jnp.bfloat16)
        dv_ref[idx[j]] = dv_a[rows, :].astype(jnp.bfloat16)


def attention(idx, q, rk, rv, da):
    tokens, columns = q.shape
    keys = idx.shape[0] * BLOCK
    vm = pl.BlockSpec(memory_space=pltpu.VMEM)
    bf, f32 = jnp.bfloat16, jnp.float32
    return pl.pallas_call(
        attention_kernel,
        out_shape=(
            jax.ShapeDtypeStruct((tokens, columns), bf),
            jax.ShapeDtypeStruct((tokens, columns), bf),
            jax.ShapeDtypeStruct(rk.shape, bf),
            jax.ShapeDtypeStruct(rv.shape, bf),
        ),
        in_specs=[pl.BlockSpec(memory_space=pltpu.SMEM), vm, vm, vm, vm],
        out_specs=(vm, vm, vm, vm),
        scratch_shapes=[
            pltpu.VMEM((keys, columns), bf),
            pltpu.VMEM((keys, columns), bf),
            pltpu.VMEM((columns, keys), bf),
            pltpu.VMEM((columns, keys), bf),
            pltpu.VMEM((keys, QB), f32),
            pltpu.VMEM((keys, QB), bf),
            pltpu.VMEM((keys, columns), f32),
            pltpu.VMEM((keys, columns), f32),
        ],
        compiler_params=pltpu.CompilerParams(vmem_limit_bytes=40 * 2**20),
        name="attention",
    )(idx, q, rk, rv, da)


def scatter_kernel(chosen, filled, gk_ref, gv_ref, ok_ref, ov_ref, ak, av):
    ak[...] = jnp.zeros_like(ak)
    av[...] = jnp.zeros_like(av)
    for v in range(gk_ref.shape[0]):
        @pl.when(filled[v] != 0)
        def _():
            b = chosen[v]
            ak[b] = ak[b] + gk_ref[v].astype(jnp.float32)
            av[b] = av[b] + gv_ref[v].astype(jnp.float32)
    ok_ref[...] = ak[...].astype(jnp.bfloat16)
    ov_ref[...] = av[...].astype(jnp.bfloat16)


def scatter(chosen, filled, gk, gv, blocks):
    columns = gk.shape[2]
    vm = pl.BlockSpec(memory_space=pltpu.VMEM)
    sm = pl.BlockSpec(memory_space=pltpu.SMEM)
    out = jax.ShapeDtypeStruct((blocks, BLOCK, columns), jnp.bfloat16)
    return pl.pallas_call(
        scatter_kernel,
        out_shape=(out, out),
        in_specs=[sm, sm, vm, vm],
        out_specs=(vm, vm),
        scratch_shapes=[pltpu.VMEM((blocks, BLOCK, columns), jnp.float32)] * 2,
        name="scatter",
    )(chosen, filled, gk, gv)


def body(query_rows, key_rows, value_rows, out_weight, out_grad, source_view, source_block):
    tokens, columns = query_rows.shape
    blocks = tokens // BLOCK
    view = lax.axis_index("view")
    head = lax.axis_index("head")
    matched = source_view == view
    filled = jnp.any(matched, axis=1).astype(jnp.int32)
    chosen = jnp.sum(jnp.where(matched, source_block, 0), axis=1)
    own_view = lax.dynamic_index_in_dim(source_view, view, 0, keepdims=False)

    def fetch(rows):
        out = jnp.take(rows.reshape(blocks, BLOCK, columns), chosen, axis=0)
        return lax.all_to_all(out, "view", split_axis=0, concat_axis=0, tiled=True)

    rk = fetch(key_rows)
    rv = fetch(value_rows)
    og = lax.all_gather(out_grad, "head", axis=1, tiled=True)
    w_rows = lax.dynamic_slice_in_dim(out_weight, head * columns, columns, 0)
    da = lax.dot_general(
        og, w_rows, (((1,), (1,)), ((), ())), preferred_element_type=jnp.float32
    ).astype(jnp.bfloat16)
    att, dq, dk, dv = attention(own_view, query_rows, rk, rv, da)
    gk = lax.all_to_all(dk, "view", split_axis=0, concat_axis=0, tiled=True)
    gv = lax.all_to_all(dv, "view", split_axis=0, concat_axis=0, tiled=True)
    full = lax.all_gather(att, "head", axis=1, tiled=True)
    w_cols = lax.dynamic_slice_in_dim(out_weight, head * columns, columns, 1)
    mixed = dot(full, w_cols).astype(jnp.bfloat16)
    kg, vg = scatter(chosen, filled, gk, gv, blocks)
    return mixed, dq, kg.reshape(tokens, columns), vg.reshape(tokens, columns)


def solution(mesh):
    placed = (
        P("view", "head"),
        P("view", "head"),
        P("view", "head"),
        P(),
        P("view", "head"),
        P(),
        P(),
    )
    return jax.shard_map(
        body,
        mesh=mesh,
        in_specs=placed,
        out_specs=(P("view", "head"), P("view", "head"), P("view", "head"), P("view", "head")),
        check_vma=False,
    )
```

time: 225 us -> 190 us (0.84)
  local copies, waits for them, and re-layouts: 39.9 us -> 5.57 us
  matrix products: 33.4 us -> 5.32 us
  Pallas kernels: 0 us -> 25.2 us
  between operations: 0.99 us -> 14.2 us
  other arithmetic: 14.6 us -> 4.95 us
    dot_general x18 -> x2, matrix products: 33.4 us -> 5.32 us  [the longest x1 3.01 us: dot(): return jnp.dot(a, b, preferred_element_type=jnp.float32)]
    pallas_call x0 -> x2, Pallas kernels: none -> 25.2 us  [the longest x1 22.2 us: attention(): pl.pallas_call(attention_kernel, out_shape=(jax.ShapeDtypeStruct((tokens,...]
    unnamed x37 -> x14, local copies, waits for them, and re-layouts: 8.67 us -> 1.99 us
    reshape x5 -> x0, local copies, waits for them, and re-layouts: 6.12 us -> none  [the longest x1 1.85 us: body(): attended_grad.astype(jnp.bfloat16)]
    slice x4 -> x0, local copies, waits for them, and re-layouts: 6.02 us -> none  [the longest x2 3.12 us: body(): value_heads = fetched[:, columns:].reshape(key_count, heads_here, HEAD_DIM)]
    while x40 -> x0, local copies, waits for them, and re-layouts: 5.75 us -> none
    reduce_sum x5 -> x1, other arithmetic: 5.38 us -> 0.72 us  [body(): chosen = jnp.sum(jnp.where(matched, source_block, 0), axis=1)]
    all_to_all x4, waiting for transfers between devices: 106 us -> 103 us  [the longest x2 51.7 us: fetch(): return lax.all_to_all(out, 'view', split_axis=0, concat_axis=0, tiled=True)]
  transfers between devices with their start and end apart: 4 -> 6, of which waited for: 3 -> 4; matrix products, arithmetic and copies ran while one was open for 23% -> 2% of each run, Pallas kernels for 0% -> 2%
where the time goes in v1:
time: 190 us; the launch traced here: 189 us
  waiting for transfers between devices  105 us (55%)
  starting transfers between devices  28.7 us (15%)
  Pallas kernels  25.2 us (13%)
  between operations  14.2 us (7%)
  local copies, waits for them, and re-layouts  5.57 us (3%)
  matrix products  5.32 us (3%)
  other arithmetic  4.95 us (3%)
    all_to_all x2, waiting for transfers between devices, fetch(): return lax.all_to_all(out, 'view', split_axis=0, concat_axis=0, tiled=True)  51.7 us
    all_to_all x1, waiting for transfers between devices, body(): gv = lax.all_to_all(dv, 'view', split_axis=0, concat_axis=0, tiled=True)  25.9 us
    all_to_all x1, waiting for transfers between devices, body(): gk = lax.all_to_all(dk, 'view', split_axis=0, concat_axis=0, tiled=True)  25.9 us
    pallas_call x1, Pallas kernels, attention(): pl.pallas_call(attention_kernel, out_shape=(jax.ShapeDtypeStruct((tokens,...  22.2 us
    all_to_all x2, starting transfers between devices, fetch(): return lax.all_to_all(out, 'view', split_axis=0, concat_axis=0, tiled=True)  17.3 us
    all_to_all x1, starting transfers between devices, body(): gv = lax.all_to_all(dv, 'view', split_axis=0, concat_axis=0, tiled=True)  5.72 us
    all_to_all x1, starting transfers between devices, body(): gk = lax.all_to_all(dk, 'view', split_axis=0, concat_axis=0, tiled=True)  5.59 us
  transfers between devices with their start and end apart: 6, of which 4 were waited for; matrix products, arithmetic and copies ran while one was open for 2% of the time, Pallas kernels for 2%

profile of v1, /device:TPU:2, one launch (start us, length us, event | category | flops | bytes accessed | tf_op | source)
XLA Modules:
  0.0 188.8 jit_solution(11027217328336410398)
XLA Ops:
  7.2 0.0 copy-start
  7.2 0.0 copy-start.3
  7.2 0.9 fusion.5
  8.1 0.7 select_reduce_fusion.chosen
  8.8 0.0 copy-start.6
  8.8 1.7 gather_fusion.1
  10.5 0.0 copy-done.3
  10.6 1.7 gather_fusion
  12.2 0.0 copy-done.6
  12.3 2.8 %broadcast_select_fusion = (bf16[32,128,128]{2,1,0:T(8,128)(2,1)}, bf16[32,128,128]{2,1,0:T(8,128)(2,1)}) fusion(bf16[32,128,128]{2,1,0:T(8,128)(2,1)S(1)} %gather_fusion.1, pred[32]{0:T(512)(128)(4,1)S(1)} %compare_and_fusion, bf16[32,128,128]{2,1,0:T(8,128)(2,1)} %gather_fusion), kind=kLoop, calls=%fused_computation.5 | loop fusion | flops 1048576 | bytes 4194336 | tf_op jit(solution)/shard_map/jit(_take)/select_n | solution.py:171
  15.1 0.0 copy-start.5
  15.1 11.6 %all-to-all-start.1 = ((bf16[32,128,128]{2,1,0:T(8,128)(2,1)}), bf16[32,128,128]{2,1,0:T(8,128)(2,1)S(1)}, u32[]{:S(2)}, u32[]{:S(2)}) async-start(bf16[32,128,128]{2,1,0:T(8,128)(2,1)} %get-tuple-element.19), calls=%async_computation.1 | async-start | bytes 2097152 | tf_op jit(solution)/shard_map/all_to_all | solution.py:172
  26.7 0.0 all-gather.3.cloned.1.call-start
  26.7 0.7 all-gather.3.cloned.1.call-update
  27.4 27.3 %all-to-all-done.1.rv_ref = bf16[32,128,128]{2,1,0:T(8,128)(2,1)S(1)} async-done(((bf16[32,128,128]{2,1,0:T(8,128)(2,1)}), bf16[32,128,128]{2,1,0:T(8,128)(2,1)S(1)}, u32[]{:S(2)}, u32[]{:S(2)}) %all-to-all-start.1) | async-done | bytes 1048608 | tf_op jit(solution)/shard_map/all_to_all | solution.py:172
  54.7 5.7 %all-to-all-start = ((bf16[32,128,128]{2,1,0:T(8,128)(2,1)}), bf16[32,128,128]{2,1,0:T(8,128)(2,1)}, u32[]{:S(2)}, u32[]{:S(2)}) async-start(bf16[32,128,128]{2,1,0:T(8,128)(2,1)} %get-tuple-element.20), calls=%async_computation | async-start | bytes 2097152 | tf_op jit(solution)/shard_map/all_to_all | solution.py:172
  60.5 0.0 copy-done.5
  60.5 0.2 dynamic-slice_reduce_fusion.idx
  60.7 0.0 all-gather.3.cloned.1.call-done
  60.7 0.0 copy-done
  60.7 2.3 %fusion.da_ref = bf16[1024,128]{1,0:T(8,128)(2,1)S(1)} fusion(bf16[1024,1024]{1,0:T(8,128)(2,1)} %all-gather.3.cloned.1.call-done, bf16[1024,1024]{1,0:T(8,128)(2,1)S(1)} %copy-done, s32[]{:T(128)S(6)} %select_n.21), kind=kOutput, calls=%fused_computation.4 | convolution fusion | flops 268566528 | bytes 2621444 | tf_op jit(solution)/shard_map/dot_general | solution.py:178
  63.0 24.4 %all-to-all-done.rk_ref = bf16[32,128,128]{2,1,0:T(8,128)(2,1)} async-done(((bf16[32,128,128]{2,1,0:T(8,128)(2,1)}), bf16[32,128,128]{2,1,0:T(8,128)(2,1)}, u32[]{:S(2)}, u32[]{:S(2)}) %all-to-all-start) | async-done | bytes 1048608 | tf_op jit(solution)/shard_map/all_to_all | solution.py:172
  87.4 0.0 copy-start.2
  87.4 0.9 copy-done.2
  88.4 22.2 %attention.1 = (bf16[1024,128]{1,0:T(8,128)(2,1)}, bf16[1024,128]{1,0:T(8,128)(2,1)}, bf16[32,128,128]{2,1,0:T(8,128)(2,1)S(1)}, bf16[32,128,128]{2,1,0:T(8,128)(2,1)}) custom-call(s32[16]{0:T(128)S(1)} %dynamic-slice_reduce_fusion.idx, bf16[1024,128]{1,0:T(8,128)(2,1)S(1)} %copy-done.2, bf16[32,128,128]{2,1,0:T(8,128)(2,1)} %all-to-all-done.rk_ref, ...), custom_call_target="tpu_custom_call" | custom-call | tf_op jit(solution)/shard_map/attention/pallas_call | solution.py:107
  110.6 0.0 copy-start.1
  110.6 1.0 copy-done.1
  111.6 5.6 %all-to-all-start.2 = ((bf16[32,128,128]{2,1,0:T(8,128)(2,1)}), bf16[32,128,128]{2,1,0:T(8,128)(2,1)S(1)}, u32[]{:S(2)}, u32[]{:S(2)}) async-start(bf16[32,128,128]{2,1,0:T(8,128)(2,1)} %copy-done.1), calls=%async_computation.2 | async-start | bytes 2097152 | tf_op jit(solution)/shard_map/all_to_all | solution.py:182
  117.2 0.0 all-gather.5.cloned.1.call-start
  117.2 0.7 all-gather.5.cloned.1.call-update
  117.9 25.9 %all-to-all-done.2.gk_ref = bf16[32,128,128]{2,1,0:T(8,128)(2,1)S(1)} async-done(((bf16[32,128,128]{2,1,0:T(8,128)(2,1)}), bf16[32,128,128]{2,1,0:T(8,128)(2,1)S(1)}, u32[]{:S(2)}, u32[]{:S(2)}) %all-to-all-start.2) | async-done | bytes 1048608 | tf_op jit(solution)/shard_map/all_to_all | solution.py:182
  143.8 0.0 copy-start.4
  143.8 5.7 %all-to-all-start.3 = ((bf16[32,128,128]{2,1,0:T(8,128)(2,1)}), bf16[32,128,128]{2,1,0:T(8,128)(2,1)}, u32[]{:S(2)}, u32[]{:S(2)}) async-start(bf16[32,128,128]{2,1,0:T(8,128)(2,1)} %get-tuple-element.14), calls=%async_computation.3 | async-start | bytes 2097152 | tf_op jit(solution)/shard_map/all_to_all | solution.py:183
  149.5 0.5 convert_element_type.14.filled
  150.0 25.9 %all-to-all-done.3.gv_ref = bf16[32,128,128]{2,1,0:T(8,128)(2,1)} async-done(((bf16[32,128,128]{2,1,0:T(8,128)(2,1)}), bf16[32,128,128]{2,1,0:T(8,128)(2,1)}, u32[]{:S(2)}, u32[]{:S(2)}) %all-to-all-start.3) | async-done | bytes 1048608 | tf_op jit(solution)/shard_map/all_to_all | solution.py:183
  176.0 0.0 copy-done.4
  176.0 3.0 %scatter.1 = (bf16[8,128,128]{2,1,0:T(8,128)(2,1)}, bf16[8,128,128]{2,1,0:T(8,128)(2,1)}) custom-call(s32[32]{0:T(128)} %copy-done.6, s32[32]{0:T(128)} %convert_element_type.14.filled, bf16[32,128,128]{2,1,0:T(8,128)(2,1)} %copy-done.4, bf16[32,128,128]{2,1,0:T(8,128)(2,1)} %all-to-all-done.3.gv_ref), custom_call_target="tpu_custom_call" | custom-call | tf_op jit(solution)/shard_map/scatter/pallas_call | solution.py:150
  179.0 0.0 all-gather.5.cloned.1.call-done
  179.0 3.0 %convolution_convert_fusion = bf16[1024,128]{1,0:T(8,128)(2,1)} fusion(bf16[1024,1024]{1,0:T(8,128)(2,1)} %all-gather.5.cloned.1.call-done, bf16[1024,1024]{1,0:T(8,128)(2,1)S(1)} %copy-done, s32[]{:T(128)S(6)} %select_n.21), kind=kOutput, calls=%fused_computation.2 | convolution fusion | flops 268566528 | bytes 2621444 | tf_op jit(solution)/shard_map/dot_general | solution.py:19
  (3 shorter events, 0.0 us)
Async XLA Ops:
  7.2 53.5 %copy-start = (bf16[1024,1024]{1,0:T(8,128)(2,1)S(1)}, bf16[1024,1024]{1,0:T(8,128)(2,1)}, u32[]{:S(2)}) copy-start(bf16[1024,1024]{1,0:T(8,128)(2,1)} %param.12) | copy-start | bytes 6291460
  7.2 3.4 %copy-start.3 = (bf16[1024,128]{1,0:T(8,128)(2,1)S(1)}, bf16[1024,128]{1,0:T(8,128)(2,1)}, u32[]{:S(2)}) copy-start(bf16[1024,128]{1,0:T(8,128)(2,1)} %param.10) | copy-start | bytes 786436
  8.8 3.5 %copy-start.6 = (s32[32]{0:T(128)}, s32[32]{0:T(128)S(1)}, u32[]{:S(2)}) copy-start(s32[32]{0:T(128)S(1)} %select_reduce_fusion.chosen) | copy-start | bytes 388
  15.1 45.4 %copy-start.5 = (s32[32,16]{0,1:T(8,128)S(1)}, s32[32,16]{0,1:T(8,128)}, u32[]{:S(2)}) copy-start(s32[32,16]{0,1:T(8,128)} %param.14) | copy-start | bytes 6148
  15.1 39.7 %all-to-all-start.1 = ((bf16[32,128,128]{2,1,0:T(8,128)(2,1)}), bf16[32,128,128]{2,1,0:T(8,128)(2,1)S(1)}, u32[]{:S(2)}, u32[]{:S(2)}) async-start(bf16[32,128,128]{2,1,0:T(8,128)(2,1)} %get-tuple-element.19), calls=%async_computation.1 | async-start | bytes 2097152 | tf_op jit(solution)/shard_map/all_to_all | solution.py:172
  26.7 34.0 %all-gather.3.cloned.1.call-start = ((), (), s32[]{:S(2)}) async-start(), calls=%async_computation.4 | async-start | bytes 2359296 | tf_op jit(solution)/shard_map/all_gather | solution.py:176
  54.7 32.7 %all-to-all-start = ((bf16[32,128,128]{2,1,0:T(8,128)(2,1)}), bf16[32,128,128]{2,1,0:T(8,128)(2,1)}, u32[]{:S(2)}, u32[]{:S(2)}) async-start(bf16[32,128,128]{2,1,0:T(8,128)(2,1)} %get-tuple-element.20), calls=%async_computation | async-start | bytes 2097152 | tf_op jit(solution)/shard_map/all_to_all | solution.py:172
  87.4 1.0 copy-start.2
  110.6 1.0 copy-start.1
  111.6 32.2 %all-to-all-start.2 = ((bf16[32,128,128]{2,1,0:T(8,128)(2,1)}), bf16[32,128,128]{2,1,0:T(8,128)(2,1)S(1)}, u32[]{:S(2)}, u32[]{:S(2)}) async-start(bf16[32,128,128]{2,1,0:T(8,128)(2,1)} %copy-done.1), calls=%async_computation.2 | async-start | bytes 2097152 | tf_op jit(solution)/shard_map/all_to_all | solution.py:182
  117.2 61.8 %all-gather.5.cloned.1.call-start = ((), (), s32[]{:S(2)}) async-start(), calls=%async_computation.5 | async-start | bytes 2359296 | tf_op jit(solution)/shard_map/all_gather | solution.py:184
  143.8 32.2 %copy-start.4 = (bf16[32,128,128]{2,1,0:T(8,128)(2,1)}, bf16[32,128,128]{2,1,0:T(8,128)(2,1)S(1)}, u32[]{:S(2)}) copy-start(bf16[32,128,128]{2,1,0:T(8,128)(2,1)S(1)} %all-to-all-done.2.gk_ref) | copy-start | bytes 3145732
  143.8 32.2 %all-to-all-start.3 = ((bf16[32,128,128]{2,1,0:T(8,128)(2,1)}), bf16[32,128,128]{2,1,0:T(8,128)(2,1)}, u32[]{:S(2)}, u32[]{:S(2)}) async-start(bf16[32,128,128]{2,1,0:T(8,128)(2,1)} %get-tuple-element.14), calls=%async_computation.3 | async-start | bytes 2097152 | tf_op jit(solution)/shard_map/all_to_all | solution.py:183
Sparse Core Ops, SparseCore 0:
  29.3 30.0 all-gather.2
  120.4 30.0 all-gather.4

commit v2 on v1

--- a/solution.py
+++ b/solution.py
@@ -19,8 +19,367 @@
     return jnp.dot(a, b, preferred_element_type=jnp.float32)
 
 
+MESH = pl.DeviceIdType.MESH
+NZ, NY, NX = 8, 4, 4
+NB = 8
+
+
+class Copies:
+    def __init__(self, send, recv):
+        self.send, self.recv, self.n = send, recv, 0
+
+    def make(self, src, dst, device):
+        i = self.n
+        self.n += 1
+        return pltpu.make_async_remote_copy(
+            src_ref=src,
+            dst_ref=dst,
+            send_sem=self.send.at[i],
+            recv_sem=self.recv.at[i],
+            device_id=device,
+            device_id_type=MESH,
+        )
+
+
+class Place:
+    def __init__(self):
+        view = lax.axis_index("view")
+        head = lax.axis_index("head")
+        self.view, self.head = view, head
+        self.z, self.y = view // NY, lax.rem(view, NY)
+        self.x, self.c = head // 2, lax.rem(head, 2)
+
+    def zplus(self, d):
+        return lax.rem(self.z + d + NZ, NZ)
+
+    def yplus(self, k):
+        return lax.rem(self.y + k + NY, NY)
+
+    def at_z(self, d):
+        return {"view": self.zplus(d) * NY + self.y}
+
+    def at_y(self, k):
+        return {"view": self.z * NY + self.yplus(k)}
+
+    def at_x(self, d):
+        return {"head": lax.rem(self.x + d + NX, NX) * 2 + self.c}
+
+    def partner(self):
+        return {"head": self.x * 2 + 1 - self.c}
+
+    def pick(self, table, dz, k, sz):
+        taker = self.zplus(dz) * NY + self.yplus(k)
+        return table[taker * (NZ * NY) + self.zplus(sz) * NY + self.y]
+
+    def pick_abs(self, table, dz, yd, sz):
+        taker = self.zplus(dz) * NY + yd
+        return table[taker * (NZ * NY) + self.zplus(sz) * NY + self.y]
+
+
+def greet(here, zy=True, x=True):
+    barrier = pltpu.get_barrier_semaphore()
+    peers = []
+    if zy:
+        peers += [here.at_z(1), here.at_z(-1), here.at_y(1), here.at_y(2), here.at_y(3)]
+    if x:
+        peers += [here.at_x(1), here.at_x(-1), here.partner()]
+    for peer in peers:
+        pl.semaphore_signal(barrier, inc=1, device_id=peer, device_id_type=MESH)
+    pl.semaphore_wait(barrier, len(peers))
+
+
+class Gather:
+    def __init__(self, here, copies, own, full):
+        rows = own.shape[0]
+        half = rows // 2
+        x, c = here.x, here.c
+        me = here.head
+        left = lax.rem(x + NX - 1, NX) * 2 + c
+        right = lax.rem(x + 1, NX) * 2 + c
+        far = lax.rem(x + 2, NX) * 2 + c
+        lo, hi = pl.ds(0, half), pl.ds(half, half)
+        self.own, self.full, self.me = own, full, me
+        mk = copies.make
+        self.first = [
+            mk(own, full.at[me], here.at_x(1)),
+            mk(own, full.at[me], here.at_x(-1)),
+        ]
+        self.second = [
+            mk(full.at[left, lo], full.at[left, lo], here.at_x(1)),
+            mk(full.at[right, hi], full.at[right, hi], here.at_x(-1)),
+        ]
+        self.across = [
+            mk(own, full.at[me], here.partner()),
+            mk(full.at[left], full.at[left], here.partner()),
+            mk(full.at[right], full.at[right], here.partner()),
+            mk(full.at[far], full.at[far], here.partner()),
+        ]
+
+    def step(self, n):
+        if n == 0:
+            for copy in self.first:
+                copy.start()
+            self.across[0].start()
+            self.full[self.me] = self.own[...]
+        if n == 1:
+            for copy in self.first:
+                copy.wait_recv()
+            for copy in self.second:
+                copy.start()
+            self.across[1].start()
+            self.across[2].start()
+        if n == 2:
+            for copy in self.second:
+                copy.wait_recv()
+            self.across[3].start()
+        if n == 3:
+            for copy in self.across:
+                copy.wait_recv()
+        if n == 4:
+            for copy in self.first + self.second + self.across:
+                copy.wait_send()
+
+
+FETCH_PIECES = ((0, 1), (1, 3), (3, 5), (5, 8))
+
+
+class Fetch:
+    scratch = ((8, 2), (8, 2), (6, 2), (2, 2), (6, 2), (NB, 3))
+
+    def __init__(self, here, copies, table, own, got, bufs):
+        self.here, self.table, self.own, self.got = here, table, own, got
+        one, two, three, four, fwd, stage = bufs
+        self.one, self.two, self.three, self.four = one, two, three, four
+        self.fwd, self.stage = fwd, stage
+        mk = copies.make
+        ways = (here.at_z(1), here.at_z(-1))
+        h = NB // 2
+        self.c1, self.c2, self.c3, self.c4 = [], [], [], []
+        for part in range(2):
+            for s, way in enumerate(ways):
+                self.c1.append(mk(own.at[pl.ds(part * h, h)], one.at[s, pl.ds(part * h, h)], way))
+        for part in range(2):
+            for s, way in enumerate(ways):
+                self.c2.append(
+                    mk(one.at[s, pl.ds(part * h, h)], two.at[s, pl.ds(part * h, h)], way)
+                )
+        for s, way in enumerate(ways):
+            self.c3.append(mk(fwd.at[s], three.at[s], way))
+        for s, way in enumerate(ways):
+            self.c4.append(mk(three.at[s, pl.ds(4, 2)], four.at[s], way))
+        self.cy = []
+        for a, b in FETCH_PIECES:
+            self.cy.append(
+                [
+                    mk(stage.at[k - 1, pl.ds(a, b - a)], got.at[k, pl.ds(a, b - a)], here.at_y(k))
+                    for k in (2, 1, 3)
+                ]
+            )
+
+    def put(self, k, e, value):
+        if k == 0:
+            self.got[0, e] = value
+        else:
+            self.stage[k - 1, e] = value
+
+    def select(self, src, k, sz):
+        return src[jnp.maximum(self.here.pick(self.table, 0, k, sz), 0)]
+
+    def start_y(self, piece):
+        for copy in self.cy[piece]:
+            copy.start()
+
+    def step(self, n):
+        here, table = self.here, self.table
+        if n == 0:
+            for copy in self.c1:
+                copy.start()
+            for k in range(NY):
+                self.put(k, 0, self.select(self.own, k, 0))
+            self.start_y(0)
+        if n in (1, 2):
+            part = n - 1
+            for s in range(2):
+                self.c1[part * 2 + s].wait_recv()
+                self.c2[part * 2 + s].start()
+        if n == 2:
+            for k in range(NY):
+                self.put(k, 1, self.select(self.one.at[0], k, -1))
+                self.put(k, 2, self.select(self.one.at[1], k, 1))
+            self.start_y(1)
+        if n == 3:
+            for copy in self.c2:
+                copy.wait_recv()
+            for s, d in ((0, 1), (1, -1)):
+                src = self.two.at[s]
+                for yd in range(4):
+                    b = jnp.maximum(here.pick_abs(table, d, yd, -2 * d), 0)
+                    self.fwd[s, yd] = src[b]
+                for i in range(2):
+                    b = jnp.maximum(here.pick_abs(table, 2 * d, 2 * s + i, -2 * d), 0)
+                    self.fwd[s, 4 + i] = src[b]
+            for k in range(NY):
+                self.put(k, 3, self.select(self.two.at[0], k, -2))
+                self.put(k, 4, self.select(self.two.at[1], k, 2))
+            for copy in self.c3:
+                copy.start()
+            self.start_y(2)
+        if n == 4:
+            for s in range(2):
+                self.c3[s].wait_recv()
+                self.c4[s].start()
+            for k in range(NY):
+                yd = here.yplus(k)
+                self.put(k, 5, self.three[0, yd])
+                self.put(k, 6, self.three[1, yd])
+        if n == 5:
+            for copy in self.c4:
+                copy.wait_recv()
+            for k in range(NY):
+                yd = here.yplus(k)
+                low = lax.rem(yd, 2)
+                self.put(k, 7, jnp.where(yd < 2, self.four[0, low], self.four[1, low]))
+            self.start_y(3)
+        if n == 6:
+            for piece in self.cy:
+                for copy in piece:
+                    copy.wait_recv()
+        if n == 7:
+            for copy in self.c1 + self.c2 + self.c3 + self.c4:
+                copy.wait_send()
+            for piece in self.cy:
+                for copy in piece:
+                    copy.wait_send()
+
+
+RETURN_PIECES = ((5, 8), (3, 5), (1, 3), (0, 1))
+
+
+class Return:
+    scratch = ((2, 2), (6, 2), (8, 2), (8, 2), (8, 2), (8, 2))
+
+    def __init__(self, here, copies, table, sent, held, out, bufs):
+        self.here, self.table, self.held, self.out = here, table, held, out
+        four, three, two, one, out2, out1 = bufs
+        self.four, self.three, self.two, self.one = four, three, two, one
+        self.out2, self.out1 = out2, out1
+        mk = copies.make
+        ways = (here.at_z(-1), here.at_z(1))
+        h = NB // 2
+        self.cy = []
+        for a, b in RETURN_PIECES:
+            self.cy.append(
+                [
+                    mk(sent.at[k - 1, pl.ds(a, b - a)], held.at[k, pl.ds(a, b - a)], here.at_y(-k))
+                    for k in (2, 1, 3)
+                ]
+            )
+        self.c4, self.c3, self.c2, self.c1 = [], [], [], []
+        for s, way in enumerate(ways):
+            for i in range(2):
+                k = lax.rem(2 * s + i + NY - here.y, NY)
+                self.c4.append(mk(held.at[k, 7], four.at[s, i], way))
+        for s, way in enumerate(ways):
+            self.c3.append(mk(held.at[:, 5 + s], three.at[s, pl.ds(0, 4)], way))
+        for s, way in enumerate(ways):
+            self.c3.append(mk(four.at[s], three.at[s, pl.ds(4, 2)], way))
+        for part in range(2):
+            for s, way in enumerate(ways):
+                self.c2.append(
+                    mk(out2.at[s, pl.ds(part * h, h)], two.at[s, pl.ds(part * h, h)], way)
+                )
+        for part in range(2):
+            for s, way in enumerate(ways):
+                self.c1.append(
+                    mk(out1.at[s, pl.ds(part * h, h)], one.at[s, pl.ds(part * h, h)], way)
+                )
+
+    def start_y(self, piece):
+        for copy in self.cy[piece]:
+            copy.start()
+
+    def wait_y(self, piece):
+        for copy in self.cy[piece]:
+            copy.wait_recv()
+
+    @staticmethod
+    def total(b, bases, terms):
+        acc = None
+        for value in bases:
+            value = value.astype(jnp.float32)
+            acc = value if acc is None else acc + value
+        for pick, ref in terms:
+            value = ref[...].astype(jnp.float32)
+            value = jnp.where(pick == b, value, jnp.zeros_like(value))
+            acc = value if acc is None else acc + value
+        return acc.astype(jnp.bfloat16)
+
+    def here_terms(self, e, sz):
+        return [
+            (self.here.pick(self.table, 0, k, sz), self.held.at[k, e]) for k in range(NY)
+        ]
+
+    def step(self, n):
+        here, table = self.here, self.table
+        h = NB // 2
+        if n == 0:
+            for piece in range(4):
+                self.start_y(piece)
+        if n == 1:
+            self.wait_y(0)
+            for copy in self.c4 + self.c3[:2]:
+                copy.start()
+        if n == 2:
+            for copy in self.c4:
+                copy.wait_recv()
+            for copy in self.c3[2:]:
+                copy.start()
+        if n == 3:
+            self.wait_y(1)
+            for copy in self.c3:
+                copy.wait_recv()
+            for part in range(2):
+                for s, d in ((0, 1), (1, -1)):
+                    terms = self.here_terms(3 + s, -2 * d)
+                    for k in range(4):
+                        terms.append((here.pick(table, d, k, -2 * d), self.three.at[s, k]))
+                    for i in range(2):
+                        pick = here.pick_abs(table, 2 * d, 2 * s + i, -2 * d)
+                        terms.append((pick, self.three.at[s, 4 + i]))
+                    for b in range(part * h, part * h + h):
+                        self.out2[s, b] = self.total(b, [], terms)
+                for s in range(2):
+                    self.c2[part * 2 + s].start()
+        if n in (4, 5):
+            part = n - 4
+            if n == 4:
+                self.wait_y(2)
+            for s, d in ((0, 1), (1, -1)):
+                self.c2[part * 2 + s].wait_recv()
+                terms = self.here_terms(1 + s, -d)
+                for b in range(part * h, part * h + h):
+                    self.out1[s, b] = self.total(b, [self.two[s, b]], terms)
+            for s in range(2):
+                self.c1[part * 2 + s].start()
+        if n in (6, 7):
+            part = n - 6
+            if n == 6:
+                self.wait_y(3)
+            for s in range(2):
+                self.c1[part * 2 + s].wait_recv()
+            terms = self.here_terms(0, 0)
+            for b in range(part * h, part * h + h):
+                self.out[b] = self.total(b, [self.one[0, b], self.one[1, b]], terms)
+        if n == 8:
+            for copy in self.c4 + self.c3 + self.c2 + self.c1:
+                copy.wait_send()
+            for piece in self.cy:
+                for copy in piece:
+                    copy.wait_send()
+
+
 def attention_kernel(
-    idx, q_ref, rk_ref, rv_ref, da_ref,
+    idx, q_ref, rk_ref, rv_ref, og_ref, w_ref,
     att_ref, dq_ref, dk_ref, dv_ref,
     k_s, v_s, kt_s, vt_s, s_s, p_s, dk_a, dv_a,
 ):
@@ -43,7 +402,15 @@
     def step(i, carry):
         qrows = pl.ds(pl.multiple_of(i * QB, QB), QB)
         q = q_ref[qrows, :]
-        da = da_ref[qrows, :]
+        da = None
+        for g in range(og_ref.shape[0]):
+            cols = pl.ds(g * 2 * HEAD_DIM, 2 * HEAD_DIM)
+            part = lax.dot_general(
+                og_ref[g, qrows, :], w_ref[:, cols], (((1,), (1,)), ((), ())),
+                preferred_element_type=jnp.float32,
+            )
+            da = part if da is None else da + part
+        da = da.astype(jnp.bfloat16)
         qt = q.T
         dat = da.T
         atts = []
@@ -99,7 +466,7 @@
         dv_ref[idx[j]] = dv_a[rows, :].astype(jnp.bfloat16)
 
 
-def attention(idx, q, rk, rv, da):
+def attention(idx, q, rk, rv, og, w_rows):
     tokens, columns = q.shape
     keys = idx.shape[0] * BLOCK
     vm = pl.BlockSpec(memory_space=pltpu.VMEM)
@@ -112,7 +479,7 @@
             jax.ShapeDtypeStruct(rk.shape, bf),
             jax.ShapeDtypeStruct(rv.shape, bf),
         ),
-        in_specs=[pl.BlockSpec(memory_space=pltpu.SMEM), vm, vm, vm, vm],
+        in_specs=[pl.BlockSpec(memory_space=pltpu.SMEM), vm, vm, vm, vm, vm],
         out_specs=(vm, vm, vm, vm),
         scratch_shapes=[
             pltpu.VMEM((keys, columns), bf),
@@ -126,82 +493,169 @@
         ],
         compiler_params=pltpu.CompilerParams(vmem_limit_bytes=40 * 2**20),
         name="attention",
-    )(idx, q, rk, rv, da)
-
-
-def scatter_kernel(chosen, filled, gk_ref, gv_ref, ok_ref, ov_ref, ak, av):
-    ak[...] = jnp.zeros_like(ak)
-    av[...] = jnp.zeros_like(av)
-    for v in range(gk_ref.shape[0]):
-        @pl.when(filled[v] != 0)
-        def _():
-            b = chosen[v]
-            ak[b] = ak[b] + gk_ref[v].astype(jnp.float32)
-            av[b] = av[b] + gv_ref[v].astype(jnp.float32)
-    ok_ref[...] = ak[...].astype(jnp.bfloat16)
-    ov_ref[...] = av[...].astype(jnp.bfloat16)
-
-
-def scatter(chosen, filled, gk, gv, blocks):
-    columns = gk.shape[2]
+    )(idx, q, rk, rv, og, w_rows)
+
+
+def fetch_kernel(table, og_ref, k_ref, v_ref, gk_ref, gv_ref, full_ref, *scratch):
+    bk, bv, (send, recv) = scratch[:6], scratch[6:12], scratch[12:]
+    here = Place()
+    copies = Copies(send, recv)
+    og = Gather(here, copies, og_ref, full_ref)
+    fk = Fetch(here, copies, table, k_ref, gk_ref, bk)
+    fv = Fetch(here, copies, table, v_ref, gv_ref, bv)
+    greet(here)
+    fk.step(0)
+    og.step(0)
+    fv.step(0)
+    fk.step(1)
+    fk.step(2)
+    fv.step(1)
+    fv.step(2)
+    og.step(1)
+    fk.step(3)
+    fk.step(4)
+    fv.step(3)
+    og.step(2)
+    fk.step(5)
+    fv.step(4)
+    fv.step(5)
+    og.step(3)
+    fk.step(6)
+    fv.step(6)
+    fk.step(7)
+    fv.step(7)
+    og.step(4)
+
+
+def fetch_scratch():
+    return [pltpu.VMEM((b, a, BLOCK, 2 * HEAD_DIM), jnp.bfloat16) for a, b in Fetch.scratch]
+
+
+def fetch(table, og, k, v):
+    bf = jnp.bfloat16
+    tokens, columns = og.shape
     vm = pl.BlockSpec(memory_space=pltpu.VMEM)
-    sm = pl.BlockSpec(memory_space=pltpu.SMEM)
-    out = jax.ShapeDtypeStruct((blocks, BLOCK, columns), jnp.bfloat16)
+    got = jax.ShapeDtypeStruct((NY, NZ, BLOCK, columns), bf)
     return pl.pallas_call(
-        scatter_kernel,
-        out_shape=(out, out),
-        in_specs=[sm, sm, vm, vm],
-        out_specs=(vm, vm),
-        scratch_shapes=[pltpu.VMEM((blocks, BLOCK, columns), jnp.float32)] * 2,
-        name="scatter",
-    )(chosen, filled, gk, gv)
+        fetch_kernel,
+        out_shape=(got, got, jax.ShapeDtypeStruct((2 * NX, tokens, columns), bf)),
+        in_specs=[pl.BlockSpec(memory_space=pltpu.SMEM), vm, vm, vm],
+        out_specs=(vm, vm, vm),
+        scratch_shapes=fetch_scratch() + fetch_scratch()
+        + [pltpu.SemaphoreType.DMA((64,)), pltpu.SemaphoreType.DMA((64,))],
+        compiler_params=pltpu.CompilerParams(
+            collective_id=0, has_side_effects=True, vmem_limit_bytes=40 * 2**20
+        ),
+        name="fetch",
+    )(table, og, k, v)
+
+
+def return_kernel(table, att_ref, w_ref, ck_ref, cv_ref, mixed_ref, ok_ref, ov_ref, *scratch):
+    bk, bv = scratch[:6], scratch[6:12]
+    full, hk, hv, send, recv = scratch[12:]
+    here = Place()
+    copies = Copies(send, recv)
+    hk[0] = ck_ref[0]
+    hv[0] = cv_ref[0]
+    at = Gather(here, copies, att_ref, full)
+    rk = Return(here, copies, table, ck_ref.at[pl.ds(1, 3)], hk, ok_ref, bk)
+    rv = Return(here, copies, table, cv_ref.at[pl.ds(1, 3)], hv, ov_ref, bv)
+    greet(here)
+    rk.step(0)
+    rv.step(0)
+    at.step(0)
+    rk.step(1)
+    rk.step(2)
+    rv.step(1)
+    rv.step(2)
+    at.step(1)
+    rk.step(3)
+    at.step(2)
+    rv.step(3)
+    at.step(3)
+
+    def mix(i, carry):
+        rows = pl.ds(pl.multiple_of(i * QB, QB), QB)
+        acc = None
+        for g in range(2 * NX):
+            part = dot(full[g, rows, :], w_ref[pl.ds(g * 2 * HEAD_DIM, 2 * HEAD_DIM), :])
+            acc = part if acc is None else acc + part
+        mixed_ref[rows, :] = acc.astype(jnp.bfloat16)
+        return carry
+
+    lax.fori_loop(0, mixed_ref.shape[0] // QB, mix, 0)
+    rk.step(4)
+    rk.step(5)
+    rv.step(4)
+    rv.step(5)
+    rk.step(6)
+    rk.step(7)
+    rv.step(6)
+    rv.step(7)
+    rk.step(8)
+    rv.step(8)
+    at.step(4)
+
+
+def give_back(table, att, w_cols, ck, cv):
+    bf = jnp.bfloat16
+    tokens, columns = att.shape
+    vm = pl.BlockSpec(memory_space=pltpu.VMEM)
+    out = jax.ShapeDtypeStruct((NB, BLOCK, columns), bf)
+    bufs = [pltpu.VMEM((b, a, BLOCK, columns), bf) for a, b in Return.scratch]
+    return pl.pallas_call(
+        return_kernel,
+        out_shape=(jax.ShapeDtypeStruct((tokens, columns), bf), out, out),
+        in_specs=[pl.BlockSpec(memory_space=pltpu.SMEM), vm, vm, vm, vm],
+        out_specs=(vm, vm, vm),
+        scratch_shapes=bufs + bufs + [
+            pltpu.VMEM((2 * NX, tokens, columns), bf),
+            pltpu.VMEM((NY, NZ, BLOCK, columns), bf),
+            pltpu.VMEM((NY, NZ, BLOCK, columns), bf),
+            pltpu.SemaphoreType.DMA((64,)),
+            pltpu.SemaphoreType.DMA((64,)),
+        ],
+        compiler_params=pltpu.CompilerParams(
+            collective_id=1, has_side_effects=True, vmem_limit_bytes=40 * 2**20
+        ),
+        name="give_back",
+    )(table, att, w_cols, ck, cv)
+
+
+def routes(source_view, source_block):
+    view = lax.axis_index("view")
+    views = jnp.arange(NZ * NY, dtype=jnp.int32)
+    same = source_view[:, :, None] == views[None, None, :]
+    table = jnp.max(jnp.where(same, source_block[:, :, None], -1), axis=1).reshape(-1)
+    mine = lax.dynamic_index_in_dim(source_view, view, 0, keepdims=False)
+    dz = lax.rem(view // NY - mine // NY + NZ, NZ)
+    dy = lax.rem(lax.rem(view, NY) - lax.rem(mine, NY) + NY, NY)
+    place = dy * NZ + jnp.where(dz == 0, 0, jnp.where(dz <= 4, 2 * dz - 1, 16 - 2 * dz))
+    return table, place
 
 
 def body(query_rows, key_rows, value_rows, out_weight, out_grad, source_view, source_block):
     tokens, columns = query_rows.shape
-    blocks = tokens // BLOCK
-    view = lax.axis_index("view")
     head = lax.axis_index("head")
-    matched = source_view == view
-    filled = jnp.any(matched, axis=1).astype(jnp.int32)
-    chosen = jnp.sum(jnp.where(matched, source_block, 0), axis=1)
-    own_view = lax.dynamic_index_in_dim(source_view, view, 0, keepdims=False)
-
-    def fetch(rows):
-        out = jnp.take(rows.reshape(blocks, BLOCK, columns), chosen, axis=0)
-        return lax.all_to_all(out, "view", split_axis=0, concat_axis=0, tiled=True)
-
-    rk = fetch(key_rows)
-    rv = fetch(value_rows)
-    og = lax.all_gather(out_grad, "head", axis=1, tiled=True)
+    table, place = routes(source_view, source_block)
+    cut = (NB, BLOCK, columns)
+    got_k, got_v, og = fetch(table, out_grad, key_rows.reshape(cut), value_rows.reshape(cut))
+    flat = (NY * NZ, BLOCK, columns)
     w_rows = lax.dynamic_slice_in_dim(out_weight, head * columns, columns, 0)
-    da = lax.dot_general(
-        og, w_rows, (((1,), (1,)), ((), ())), preferred_element_type=jnp.float32
-    ).astype(jnp.bfloat16)
-    att, dq, dk, dv = attention(own_view, query_rows, rk, rv, da)
-    gk = lax.all_to_all(dk, "view", split_axis=0, concat_axis=0, tiled=True)
-    gv = lax.all_to_all(dv, "view", split_axis=0, concat_axis=0, tiled=True)
-    full = lax.all_gather(att, "head", axis=1, tiled=True)
     w_cols = lax.dynamic_slice_in_dim(out_weight, head * columns, columns, 1)
-    mixed = dot(full, w_cols).astype(jnp.bfloat16)
-    kg, vg = scatter(chosen, filled, gk, gv, blocks)
+    att, dq, ck, cv = attention(
+        place, query_rows, got_k.reshape(flat), got_v.reshape(flat), og, w_rows
+    )
+    mixed, kg, vg = give_back(table, att, w_cols, ck.reshape(got_k.shape), cv.reshape(got_v.shape))
     return mixed, dq, kg.reshape(tokens, columns), vg.reshape(tokens, columns)
 
 
 def solution(mesh):
-    placed = (
-        P("view", "head"),
-        P("view", "head"),
-        P("view", "head"),
-        P(),
-        P("view", "head"),
-        P(),
-        P(),
-    )
+    spread = P("view", "head")
     return jax.shard_map(
         body,
         mesh=mesh,
-        in_specs=placed,
-        out_specs=(P("view", "head"), P("view", "head"), P("view", "head"), P("view", "head")),
+        in_specs=(spread, spread, spread, P(), spread, P(), P()),
+        out_specs=(spread, spread, spread, spread),
         check_vma=False,
     )

time: 190 us -> 137 us (0.72)
  waiting for transfers between devices: 105 us -> 0 us
  Pallas kernels: 25.2 us -> 126 us
  starting transfers between devices: 28.7 us -> 0 us
  between operations: 14.2 us -> 0.71 us
  matrix products: 5.32 us -> 0 us
  other arithmetic: 4.95 us -> 0.25 us
  local copies, waits for them, and re-layouts: 5.57 us -> 9.16 us
    all_to_all x4 -> x0, waiting for transfers between devices: 103 us -> none  [the longest x2 51.7 us: fetch(): return lax.all_to_all(out, 'view', split_axis=0, concat_axis=0, tiled=True)]
    pallas_call x1 -> x2, Pallas kernels: 3.02 us -> 104 us  [the longest x1 52.7 us: fetch(): pl.pallas_call(fetch_kernel, out_shape=(got, got, jax.ShapeDtypeStruct((2...]
    all_to_all x4 -> x0, starting transfers between devices: 28.6 us -> none  [the longest x2 17.3 us: fetch(): return lax.all_to_all(out, 'view', split_axis=0, concat_axis=0, tiled=True)]
    unnamed x14 -> x15, local copies, waits for them, and re-layouts: 1.99 us -> 7.98 us
    dot_general x2 -> x0, matrix products: 5.32 us -> none  [the longest x1 3.01 us: dot(): return jnp.dot(a, b, preferred_element_type=jnp.float32)]
    gather x2 -> x0, local copies, waits for them, and re-layouts: 3.39 us -> none  [fetch(): out = jnp.take(rows.reshape(blocks, BLOCK, columns), chosen, axis=0)]
    select_n x2 -> x0, other arithmetic: 2.82 us -> none  [fetch(): out = jnp.take(rows.reshape(blocks, BLOCK, columns), chosen, axis=0)]
  transfers between devices with their start and end apart: 6 -> 0, of which waited for: 4 -> 0; matrix products, arithmetic and copies ran while one was open for 2% -> 0% of each run, Pallas kernels for 2% -> 0%
where the time goes in v2:
time: 137 us; the launch traced here: 136 us
  Pallas kernels  126 us (92%)
  local copies, waits for them, and re-layouts  9.16 us (7%)
    pallas_call x1, Pallas kernels, fetch(): pl.pallas_call(fetch_kernel, out_shape=(got, got, jax.ShapeDtypeStruct((2...  52.7 us
    pallas_call x1, Pallas kernels, give_back(): pl.pallas_call(return_kernel, out_shape=(jax.ShapeDtypeStruct((tokens, co...  51.5 us
    pallas_call x1, Pallas kernels, attention(): pl.pallas_call(attention_kernel, out_shape=(jax.ShapeDtypeStruct((tokens,...  22.1 us
    unnamed x15, local copies, waits for them, and re-layouts  7.98 us

profile of v2, /device:TPU:2, one launch (start us, length us, event | category | flops | bytes accessed | tf_op | source)
XLA Modules:
  0.0 136.4 jit_solution(11055066855556621411)
XLA Ops:
  0.6 0.0 copy-start
  0.7 1.0 dynamic-slice_reduce_fusion
  1.7 0.5 copy-done
  2.3 0.8 copy.15
  3.0 0.8 copy.16
  3.8 0.2 select_reduce_fusion
  4.0 0.1 reshape.37.table
  4.1 0.0 copy-start.1
  4.1 0.9 copy-done.1
  5.1 0.0 copy-start.2
  5.1 0.9 copy-done.2
  6.0 0.0 copy-start.3
  6.0 0.9 copy-done.3
  7.0 52.7 %fetch.1 = (bf16[4,8,128,128]{3,2,1,0:T(8,128)(2,1)S(1)}, bf16[4,8,128,128]{3,2,1,0:T(8,128)(2,1)S(1)}, bf16[8,1024,128]{2,1,0:T(8,128)(2,1)S(1)}) custom-call(s32[1024]{0:T(1024)S(1)} %reshape.37.table, bf16[1024,128]{1,0:T(8,128)(2,1)S(1)} %copy-done.1, bf16[8,128,128]{2,1,0:T(8,128)(2,1)S(1)} %bitcast.12, bf16[8,128,128]{2,1,0:T(8,128)(2,1)S(1)} %bitcast.13), custom_call_target="tpu_custom_call" | custom-call | tf_op jit(solution)/shard_map/fetch/pallas_call | solution.py:539
  59.7 0.0 copy-start.4
  59.7 0.9 copy-done.4
  60.7 22.1 %attention.1 = (bf16[1024,128]{1,0:T(8,128)(2,1)S(1)}, bf16[1024,128]{1,0:T(8,128)(2,1)}, bf16[32,128,128]{2,1,0:T(8,128)(2,1)S(1)}, bf16[32,128,128]{2,1,0:T(8,128)(2,1)S(1)}) custom-call(s32[16]{0:T(128)S(1)} %fusion.idx, bf16[1024,128]{1,0:T(8,128)(2,1)S(1)} %copy-done.4, bf16[32,128,128]{2,1,0:T(8,128)(2,1)S(1)} %bitcast.10, ...), custom_call_target="tpu_custom_call" | custom-call | tf_op jit(solution)/shard_map/attention/pallas_call | solution.py:474
  82.7 0.1 constant_dynamic-slice_fusion.w_ref
  82.8 51.5 %give_back.1 = (bf16[1024,128]{1,0:T(8,128)(2,1)S(1)}, bf16[8,128,128]{2,1,0:T(8,128)(2,1)S(1)}, bf16[8,128,128]{2,1,0:T(8,128)(2,1)S(1)}) custom-call(s32[1024]{0:T(1024)S(1)} %reshape.37.table, bf16[1024,128]{1,0:T(8,128)(2,1)S(1)} %get-tuple-element.17.att_ref, bf16[1024,128]{1,0:T(8,128)(2,1)S(1)} %constant_dynamic-slice_fusion.w_ref, ...), custom_call_target="tpu_custom_call" | custom-call | tf_op jit(solution)/shard_map/give_back/pallas_call | solution.py:606
  134.3 0.7 copy.20
  135.0 0.7 copy.21
  135.7 0.7 copy.22
  (2 shorter events, 0.0 us)
Async XLA Ops:
  0.6 1.6 %copy-start = (bf16[1024,1024]{1,0:T(8,128)(2,1)S(1)}, bf16[1024,1024]{1,0:T(8,128)(2,1)}, u32[]{:S(2)}) copy-start(bf16[1024,1024]{1,0:T(8,128)(2,1)} %param.10) | copy-start | bytes 6291460
  4.1 1.0 copy-start.1
  5.1 0.9 copy-start.2
  6.0 0.9 copy-start.3
  59.7 1.0 copy-start.4

commit v3 on v2

--- a/solution.py
+++ b/solution.py
@@ -1,5 +1,3 @@
-import functools
-
 import jax
 import jax.numpy as jnp
 from jax import lax
@@ -9,10 +7,13 @@
 
 HEAD_DIM = 64
 BLOCK = 128
+COLS = 2 * HEAD_DIM
 SCALE = HEAD_DIM ** -0.5
 LOG2E = 1.4426950408889634
 QB = 256
 KC = 256
+BF = jnp.bfloat16
+F32 = jnp.float32
 
 
 def dot(a, b):
@@ -140,7 +141,7 @@
                 copy.wait_send()
 
 
-FETCH_PIECES = ((0, 1), (1, 3), (3, 5), (5, 8))
+FETCH_PIECES = ((0, 1), (1, 3), (3, 5), (5, 7), (7, 8))
 
 
 class Fetch:
@@ -171,14 +172,18 @@
         for a, b in FETCH_PIECES:
             self.cy.append(
                 [
-                    mk(stage.at[k - 1, pl.ds(a, b - a)], got.at[k, pl.ds(a, b - a)], here.at_y(k))
+                    mk(
+                        stage.at[k - 1, pl.ds(a, b - a)],
+                        got.at[pl.ds(k * NZ + a, b - a)],
+                        here.at_y(k),
+                    )
                     for k in (2, 1, 3)
                 ]
             )
 
     def put(self, k, e, value):
         if k == 0:
-            self.got[0, e] = value
+            self.got[e] = value
         else:
             self.stage[k - 1, e] = value
 
@@ -189,11 +194,13 @@
         for copy in self.cy[piece]:
             copy.start()
 
+    def offer(self, part):
+        for copy in self.c1[part * 2 : part * 2 + 2]:
+            copy.start()
+
     def step(self, n):
         here, table = self.here, self.table
         if n == 0:
-            for copy in self.c1:
-                copy.start()
             for k in range(NY):
                 self.put(k, 0, self.select(self.own, k, 0))
             self.start_y(0)
@@ -232,6 +239,7 @@
                 yd = here.yplus(k)
                 self.put(k, 5, self.three[0, yd])
                 self.put(k, 6, self.three[1, yd])
+            self.start_y(3)
         if n == 5:
             for copy in self.c4:
                 copy.wait_recv()
@@ -239,7 +247,7 @@
                 yd = here.yplus(k)
                 low = lax.rem(yd, 2)
                 self.put(k, 7, jnp.where(yd < 2, self.four[0, low], self.four[1, low]))
-            self.start_y(3)
+            self.start_y(4)
         if n == 6:
             for piece in self.cy:
                 for copy in piece:
@@ -378,248 +386,312 @@
                     copy.wait_send()
 
 
-def attention_kernel(
-    idx, q_ref, rk_ref, rv_ref, og_ref, w_ref,
-    att_ref, dq_ref, dk_ref, dv_ref,
-    k_s, v_s, kt_s, vt_s, s_s, p_s, dk_a, dv_a,
+def rows_at(i, size):
+    return pl.ds(pl.multiple_of(i * size, size), size)
+
+
+def layer_kernel(
+    table, place, slot_of,
+    q_hbm, k_hbm, v_hbm, w_hbm, og_hbm,
+    mixed_hbm, dq_hbm, ok_hbm, ov_hbm,
+    *scratch,
 ):
-    slots = idx.shape[0]
+    fbk, fbv, rbk, rbv = scratch[:6], scratch[6:12], scratch[12:18], scratch[18:24]
+    (
+        k_own, v_own, og_own, q_s, w_rows, w_cols,
+        got_k, got_v, og_all, at_all, sent_k, sent_v, held_k, held_v,
+        qm, qtm, dam, datm, k_s, kt_s, v_s, vt_s, s_s, p_s,
+        att_t, dq_t, grad_s, att_s, dq_s, mixed_s, ok_s, ov_s,
+        send, recv, local,
+    ) = scratch[24:]
+    here = Place()
+    copies = Copies(send, recv)
+    slots = place.shape[0]
     keys = slots * BLOCK
-    tokens = q_ref.shape[0]
+    tokens = q_s.shape[0]
+    chunks = keys // KC
+    mine = pl.ds(pl.multiple_of(here.head * COLS, COLS), COLS)
+
+    loads = [
+        pltpu.make_async_copy(src, dst, local.at[i])
+        for i, (src, dst) in enumerate(
+            (
+                (k_hbm, k_own),
+                (og_hbm, og_own),
+                (v_hbm, v_own),
+                (q_hbm, q_s),
+                (w_hbm.at[mine, :], w_rows),
+                (w_hbm.at[:, mine], w_cols),
+            )
+        )
+    ]
+    stores = [
+        pltpu.make_async_copy(src, dst, local.at[len(loads) + i])
+        for i, (src, dst) in enumerate(
+            ((dq_s, dq_hbm), (mixed_s, mixed_hbm), (ov_s, ov_hbm), (ok_s, ok_hbm))
+        )
+    ]
+    for load in loads:
+        load.start()
+
+    og = Gather(here, copies, og_own, og_all)
+    fk = Fetch(here, copies, table, k_own, got_k, fbk)
+    fv = Fetch(here, copies, table, v_own, got_v, fbv)
+    at = Gather(here, copies, att_s, at_all)
+    rk = Return(here, copies, table, sent_k, held_k, ok_s, rbk)
+    rv = Return(here, copies, table, sent_v, held_v, ov_s, rbv)
+
+    greet(here)
+    loads[0].wait()
+    fk.offer(0)
+    fk.offer(1)
+    loads[1].wait()
+    og.step(0)
+    fk.step(0)
+    loads[2].wait()
+    fv.step(0)
+    loads[3].wait()
+    q = q_s[...]
+    lane = lax.broadcasted_iota(jnp.int32, q.shape, 1) // HEAD_DIM
+    for h in range(2):
+        part = jnp.where(lane == h, q, jnp.zeros_like(q))
+        qm[h] = part
+        qtm[h] = part.T
+    fk.step(1)
+    fk.step(2)
+    fv.offer(0)
+    og.step(1)
+    fk.step(3)
+    fv.offer(1)
+    og.step(2)
+    loads[4].wait()
+    og.step(3)
+
+    def project(i, carry):
+        rows = rows_at(i, QB)
+        acc = None
+        for g in range(2 * NX):
+            part = lax.dot_general(
+                og_all[g, rows, :],
+                w_rows[:, pl.ds(g * COLS, COLS)],
+                (((1,), (1,)), ((), ())),
+                preferred_element_type=jnp.float32,
+            )
+            acc = part if acc is None else acc + part
+        da = acc.astype(BF)
+        half = lax.broadcasted_iota(jnp.int32, da.shape, 1) // HEAD_DIM
+        for h in range(2):
+            part = jnp.where(half == h, da, jnp.zeros_like(da))
+            dam[h, rows, :] = part
+            datm[h, :, rows] = part.T
+        return carry
+
+    lax.fori_loop(0, tokens // QB, project, 0)
+    fk.step(4)
+    fv.step(1)
+    fk.step(5)
+    fv.step(2)
+    fk.step(6)
     for j in range(slots):
         rows = pl.ds(j * BLOCK, BLOCK)
-        kb = rk_ref[idx[j]]
-        vb = rv_ref[idx[j]]
-        k_s[rows, :] = kb
-        v_s[rows, :] = vb
-        kt_s[:, rows] = kb.T
-        vt_s[:, rows] = vb.T
-    dk_a[...] = jnp.zeros_like(dk_a)
-    dv_a[...] = jnp.zeros_like(dv_a)
-    chunks = keys // KC
-    lane = lax.broadcasted_iota(jnp.int32, (QB, 2 * HEAD_DIM), 1)
-
-    def step(i, carry):
-        qrows = pl.ds(pl.multiple_of(i * QB, QB), QB)
-        q = q_ref[qrows, :]
-        da = None
-        for g in range(og_ref.shape[0]):
-            cols = pl.ds(g * 2 * HEAD_DIM, 2 * HEAD_DIM)
-            part = lax.dot_general(
-                og_ref[g, qrows, :], w_ref[:, cols], (((1,), (1,)), ((), ())),
-                preferred_element_type=jnp.float32,
-            )
-            da = part if da is None else da + part
-        da = da.astype(jnp.bfloat16)
-        qt = q.T
-        dat = da.T
-        atts = []
-        dqs = []
-        for h in range(2):
-            hd = slice(h * HEAD_DIM, (h + 1) * HEAD_DIM)
-            mine = (lane // HEAD_DIM) == h
-            qh = jnp.where(mine, q, jnp.zeros_like(q))
-            dah = jnp.where(mine, da, jnp.zeros_like(da))
-            qth = qt[hd, :]
-            dath = dat[hd, :]
-            top = None
-            for c in range(chunks):
-                rows = pl.ds(c * KC, KC)
-                s = dot(k_s[rows, hd], qth)
-                s_s[rows, :] = s
-                m = jnp.max(s, axis=0, keepdims=True)
-                top = m if top is None else jnp.maximum(top, m)
-            shift = top * (SCALE * LOG2E)
-            total = jnp.zeros((1, QB), jnp.float32)
-            for c in range(chunks):
-                rows = pl.ds(c * KC, KC)
-                e = jnp.exp2(s_s[rows, :] * (SCALE * LOG2E) - shift)
-                s_s[rows, :] = e
-                total = total + jnp.sum(e, axis=0, keepdims=True)
-            inv = 1.0 / total
-            for c in range(chunks):
-                rows = pl.ds(c * KC, KC)
-                p = s_s[rows, :] * inv
-                pb = p.astype(jnp.bfloat16)
-                p_s[rows, :] = pb
-                dv_a[rows, :] += dot(pb, dah)
-            att = dot(vt_s[hd, :], p_s[...]).astype(jnp.bfloat16)
-            atts.append(att)
-            delta = jnp.sum(
-                att.astype(jnp.float32) * dath.astype(jnp.float32), axis=0, keepdims=True
-            )
-            for c in range(chunks):
-                rows = pl.ds(c * KC, KC)
-                dp = dot(v_s[rows, hd], dath)
-                ds = ((s_s[rows, :] * inv) * (dp - delta)).astype(jnp.bfloat16)
-                p_s[rows, :] = ds
-                dk_a[rows, :] += dot(ds, qh)
-            dqs.append(dot(kt_s[hd, :], p_s[...]) * SCALE)
-        att_ref[qrows, :] = jnp.concatenate(atts, axis=0).T
-        dq_ref[qrows, :] = jnp.concatenate(dqs, axis=0).astype(jnp.bfloat16).T
+        block = got_k[place[j]]
+        k_s[rows, :] = block
+        kt_s[:, rows] = block.T
+
+    steps = 2 * (tokens // QB)
+
+    def forward(i, carry):
+        for n, at_step in ((3, 2), (4, 6), (5, 7)):
+            @pl.when(i == at_step)
+            def _():
+                fv.step(n)
+
+        h = lax.rem(i, 2)
+        cols = rows_at(i // 2, QB)
+        qt = qtm[h, :, cols]
+        top = None
+        for c in range(chunks):
+            rows = pl.ds(c * KC, KC)
+            s = dot(k_s[rows, :], qt)
+            s_s[rows, :] = s
+            m = jnp.max(s, axis=0, keepdims=True)
+            top = m if top is None else jnp.maximum(top, m)
+        shift = top * (SCALE * LOG2E)
+        total = jnp.zeros((1, QB), F32)
+        for c in range(chunks):
+            rows = pl.ds(c * KC, KC)
+            e = jnp.exp2(s_s[rows, :] * (SCALE * LOG2E) - shift)
+            s_s[rows, :] = e
+            total = total + jnp.sum(e, axis=0, keepdims=True)
+        inv = 1.0 / total
+        for c in range(chunks):
+            rows = pl.ds(c * KC, KC)
+            p_s[h, rows, cols] = (s_s[rows, :] * inv).astype(BF)
         return carry
 
-    lax.fori_loop(0, tokens // QB, step, 0)
+    lax.fori_loop(0, steps, forward, 0)
+
+    def contract(scale, right):
+        def one(c, carry):
+            rows = rows_at(c, KC)
+            g = dot(p_s[0, rows, :], right[0]) + dot(p_s[1, rows, :], right[1])
+            if scale is not None:
+                g = g * scale
+            g = g.astype(BF)
+            for b in range(KC // BLOCK):
+                grad_s[c * (KC // BLOCK) + b] = g[b * BLOCK : (b + 1) * BLOCK, :]
+            return carry
+
+        lax.fori_loop(0, chunks, one, 0)
+
+    def hand_out(sent, held):
+        for e in range(NZ):
+            held[0, e] = grad_s[slot_of[e]]
+        for k in range(1, NY):
+            for e in range(NZ):
+                sent[k - 1, e] = grad_s[slot_of[k * NZ + e]]
+
+    contract(None, dam)
+    hand_out(sent_v, held_v)
+    rv.step(0)
+    fv.step(6)
     for j in range(slots):
         rows = pl.ds(j * BLOCK, BLOCK)
-        dk_ref[idx[j]] = (dk_a[rows, :] * SCALE).astype(jnp.bfloat16)
-        dv_ref[idx[j]] = dv_a[rows, :].astype(jnp.bfloat16)
-
-
-def attention(idx, q, rk, rv, og, w_rows):
-    tokens, columns = q.shape
-    keys = idx.shape[0] * BLOCK
-    vm = pl.BlockSpec(memory_space=pltpu.VMEM)
-    bf, f32 = jnp.bfloat16, jnp.float32
-    return pl.pallas_call(
-        attention_kernel,
-        out_shape=(
-            jax.ShapeDtypeStruct((tokens, columns), bf),
-            jax.ShapeDtypeStruct((tokens, columns), bf),
-            jax.ShapeDtypeStruct(rk.shape, bf),
-            jax.ShapeDtypeStruct(rv.shape, bf),
-        ),
-        in_specs=[pl.BlockSpec(memory_space=pltpu.SMEM), vm, vm, vm, vm, vm],
-        out_specs=(vm, vm, vm, vm),
-        scratch_shapes=[
-            pltpu.VMEM((keys, columns), bf),
-            pltpu.VMEM((keys, columns), bf),
-            pltpu.VMEM((columns, keys), bf),
-            pltpu.VMEM((columns, keys), bf),
-            pltpu.VMEM((keys, QB), f32),
-            pltpu.VMEM((keys, QB), bf),
-            pltpu.VMEM((keys, columns), f32),
-            pltpu.VMEM((keys, columns), f32),
-        ],
-        compiler_params=pltpu.CompilerParams(vmem_limit_bytes=40 * 2**20),
-        name="attention",
-    )(idx, q, rk, rv, og, w_rows)
-
-
-def fetch_kernel(table, og_ref, k_ref, v_ref, gk_ref, gv_ref, full_ref, *scratch):
-    bk, bv, (send, recv) = scratch[:6], scratch[6:12], scratch[12:]
-    here = Place()
-    copies = Copies(send, recv)
-    og = Gather(here, copies, og_ref, full_ref)
-    fk = Fetch(here, copies, table, k_ref, gk_ref, bk)
-    fv = Fetch(here, copies, table, v_ref, gv_ref, bv)
-    greet(here)
-    fk.step(0)
-    og.step(0)
-    fv.step(0)
-    fk.step(1)
-    fk.step(2)
-    fv.step(1)
-    fv.step(2)
-    og.step(1)
-    fk.step(3)
-    fk.step(4)
-    fv.step(3)
-    og.step(2)
-    fk.step(5)
-    fv.step(4)
-    fv.step(5)
-    og.step(3)
-    fk.step(6)
-    fv.step(6)
+        block = got_v[place[j]]
+        v_s[rows, :] = block
+        vt_s[:, rows] = block.T
+
+    def backward(i, carry):
+        for n, at_step in ((1, 3), (2, 5)):
+            @pl.when(i == at_step)
+            def _():
+                rv.step(n)
+
+        h = lax.rem(i, 2)
+        cols = rows_at(i // 2, QB)
+        band = rows_at(h, HEAD_DIM)
+        att = dot(vt_s[band, :], p_s[h, :, cols]).astype(BF)
+        att_t[band, cols] = att
+        delta = jnp.sum(
+            att.astype(F32) * datm[h, band, cols].astype(F32), axis=0, keepdims=True
+        )
+        dat = datm[h, :, cols]
+        for c in range(chunks):
+            rows = pl.ds(c * KC, KC)
+            dp = dot(v_s[rows, :], dat)
+            p_s[h, rows, cols] = (p_s[h, rows, cols].astype(F32) * (dp - delta)).astype(BF)
+        dq_t[band, cols] = (dot(kt_s[band, :], p_s[h, :, cols]) * SCALE).astype(BF)
+        return carry
+
+    lax.fori_loop(0, steps, backward, 0)
+    att_s[...] = att_t[...].T
+    dq_s[...] = dq_t[...].T
+    stores[0].start()
+    at.step(0)
+    contract(SCALE, qm)
+    hand_out(sent_k, held_k)
+    rk.step(0)
+    rv.step(3)
+    at.step(1)
+    rk.step(1)
+    rv.step(4)
+    rv.step(5)
+    rk.step(2)
+    at.step(2)
+    loads[5].wait()
+    rv.step(6)
+    rv.step(7)
+    stores[2].start()
+    rk.step(3)
+    at.step(3)
+
+    def mix(i, carry):
+        rows = rows_at(i, QB)
+        acc = None
+        for g in range(2 * NX):
+            part = dot(at_all[g, rows, :], w_cols[pl.ds(g * COLS, COLS), :])
+            acc = part if acc is None else acc + part
+        mixed_s[rows, :] = acc.astype(BF)
+        return carry
+
+    lax.fori_loop(0, tokens // QB, mix, 0)
+    stores[1].start()
+    rk.step(4)
+    rk.step(5)
     fk.step(7)
     fv.step(7)
     og.step(4)
-
-
-def fetch_scratch():
-    return [pltpu.VMEM((b, a, BLOCK, 2 * HEAD_DIM), jnp.bfloat16) for a, b in Fetch.scratch]
-
-
-def fetch(table, og, k, v):
-    bf = jnp.bfloat16
-    tokens, columns = og.shape
-    vm = pl.BlockSpec(memory_space=pltpu.VMEM)
-    got = jax.ShapeDtypeStruct((NY, NZ, BLOCK, columns), bf)
-    return pl.pallas_call(
-        fetch_kernel,
-        out_shape=(got, got, jax.ShapeDtypeStruct((2 * NX, tokens, columns), bf)),
-        in_specs=[pl.BlockSpec(memory_space=pltpu.SMEM), vm, vm, vm],
-        out_specs=(vm, vm, vm),
-        scratch_shapes=fetch_scratch() + fetch_scratch()
-        + [pltpu.SemaphoreType.DMA((64,)), pltpu.SemaphoreType.DMA((64,))],
-        compiler_params=pltpu.CompilerParams(
-            collective_id=0, has_side_effects=True, vmem_limit_bytes=40 * 2**20
-        ),
-        name="fetch",
-    )(table, og, k, v)
-
-
-def return_kernel(table, att_ref, w_ref, ck_ref, cv_ref, mixed_ref, ok_ref, ov_ref, *scratch):
-    bk, bv = scratch[:6], scratch[6:12]
-    full, hk, hv, send, recv = scratch[12:]
-    here = Place()
-    copies = Copies(send, recv)
-    hk[0] = ck_ref[0]
-    hv[0] = cv_ref[0]
-    at = Gather(here, copies, att_ref, full)
-    rk = Return(here, copies, table, ck_ref.at[pl.ds(1, 3)], hk, ok_ref, bk)
-    rv = Return(here, copies, table, cv_ref.at[pl.ds(1, 3)], hv, ov_ref, bv)
-    greet(here)
-    rk.step(0)
-    rv.step(0)
-    at.step(0)
-    rk.step(1)
-    rk.step(2)
-    rv.step(1)
-    rv.step(2)
-    at.step(1)
-    rk.step(3)
-    at.step(2)
-    rv.step(3)
-    at.step(3)
-
-    def mix(i, carry):
-        rows = pl.ds(pl.multiple_of(i * QB, QB), QB)
-        acc = None
-        for g in range(2 * NX):
-            part = dot(full[g, rows, :], w_ref[pl.ds(g * 2 * HEAD_DIM, 2 * HEAD_DIM), :])
-            acc = part if acc is None else acc + part
-        mixed_ref[rows, :] = acc.astype(jnp.bfloat16)
-        return carry
-
-    lax.fori_loop(0, mixed_ref.shape[0] // QB, mix, 0)
-    rk.step(4)
-    rk.step(5)
-    rv.step(4)
-    rv.step(5)
+    at.step(4)
+    rv.step(8)
     rk.step(6)
     rk.step(7)
-    rv.step(6)
-    rv.step(7)
+    stores[3].start()
     rk.step(8)
-    rv.step(8)
-    at.step(4)
-
-
-def give_back(table, att, w_cols, ck, cv):
-    bf = jnp.bfloat16
-    tokens, columns = att.shape
-    vm = pl.BlockSpec(memory_space=pltpu.VMEM)
-    out = jax.ShapeDtypeStruct((NB, BLOCK, columns), bf)
-    bufs = [pltpu.VMEM((b, a, BLOCK, columns), bf) for a, b in Return.scratch]
+    for store in stores:
+        store.wait()
+
+
+def layer(table, place, slot_of, q, k, v, w, og):
+    tokens = q.shape[0]
+    keys = place.shape[0] * BLOCK
+    hbm = pl.BlockSpec(memory_space=pl.ANY)
+    smem = pl.BlockSpec(memory_space=pltpu.SMEM)
+
+    def vmem(*shape, dtype=BF):
+        return pltpu.VMEM(shape, dtype)
+
+    def bufs(cls):
+        return [vmem(b, a, BLOCK, COLS) for a, b in cls.scratch]
+
+    rows = jax.ShapeDtypeStruct((tokens, COLS), BF)
+    cut = jax.ShapeDtypeStruct((NB, BLOCK, COLS), BF)
     return pl.pallas_call(
-        return_kernel,
-        out_shape=(jax.ShapeDtypeStruct((tokens, columns), bf), out, out),
-        in_specs=[pl.BlockSpec(memory_space=pltpu.SMEM), vm, vm, vm, vm],
-        out_specs=(vm, vm, vm),
-        scratch_shapes=bufs + bufs + [
-            pltpu.VMEM((2 * NX, tokens, columns), bf),
-            pltpu.VMEM((NY, NZ, BLOCK, columns), bf),
-            pltpu.VMEM((NY, NZ, BLOCK, columns), bf),
-            pltpu.SemaphoreType.DMA((64,)),
-            pltpu.SemaphoreType.DMA((64,)),
+        layer_kernel,
+        out_shape=(rows, rows, cut, cut),
+        in_specs=[smem, smem, smem] + [hbm] * 5,
+        out_specs=(hbm,) * 4,
+        scratch_shapes=bufs(Fetch) + bufs(Fetch) + bufs(Return) + bufs(Return) + [
+            vmem(NB, BLOCK, COLS),
+            vmem(NB, BLOCK, COLS),
+            vmem(tokens, COLS),
+            vmem(tokens, COLS),
+            vmem(COLS, w.shape[1]),
+            vmem(w.shape[0], COLS),
+            vmem(NY * NZ, BLOCK, COLS),
+            vmem(NY * NZ, BLOCK, COLS),
+            vmem(2 * NX, tokens, COLS),
+            vmem(2 * NX, tokens, COLS),
+            vmem(NY - 1, NZ, BLOCK, COLS),
+            vmem(NY - 1, NZ, BLOCK, COLS),
+            vmem(NY, NZ, BLOCK, COLS),
+            vmem(NY, NZ, BLOCK, COLS),
+            vmem(2, tokens, COLS),
+            vmem(2, COLS, tokens),
+            vmem(2, tokens, COLS),
+            vmem(2, COLS, tokens),
+            vmem(keys, COLS),
+            vmem(COLS, keys),
+            vmem(keys, COLS),
+            vmem(COLS, keys),
+            vmem(keys, QB, dtype=F32),
+            vmem(2, keys, tokens),
+            vmem(COLS, tokens),
+            vmem(COLS, tokens),
+            vmem(keys // BLOCK, BLOCK, COLS),
+            vmem(tokens, COLS),
+            vmem(tokens, COLS),
+            vmem(tokens, COLS),
+            vmem(NB, BLOCK, COLS),
+            vmem(NB, BLOCK, COLS),
+            pltpu.SemaphoreType.DMA((136,)),
+            pltpu.SemaphoreType.DMA((136,)),
+            pltpu.SemaphoreType.DMA((10,)),
         ],
         compiler_params=pltpu.CompilerParams(
-            collective_id=1, has_side_effects=True, vmem_limit_bytes=40 * 2**20
+            collective_id=0, has_side_effects=True, vmem_limit_bytes=56 * 2**20
         ),
-        name="give_back",
-    )(table, att, w_cols, ck, cv)
+        name="layer",
+    )(table, place, slot_of, q, k, v, w, og)
 
 
 def routes(source_view, source_block):
@@ -627,27 +699,23 @@
     views = jnp.arange(NZ * NY, dtype=jnp.int32)
     same = source_view[:, :, None] == views[None, None, :]
     table = jnp.max(jnp.where(same, source_block[:, :, None], -1), axis=1).reshape(-1)
-    mine = lax.dynamic_index_in_dim(source_view, view, 0, keepdims=False)
-    dz = lax.rem(view // NY - mine // NY + NZ, NZ)
-    dy = lax.rem(lax.rem(view, NY) - lax.rem(mine, NY) + NY, NY)
+    own = lax.dynamic_index_in_dim(source_view, view, 0, keepdims=False)
+    dz = lax.rem(view // NY - own // NY + NZ, NZ)
+    dy = lax.rem(lax.rem(view, NY) - lax.rem(own, NY) + NY, NY)
     place = dy * NZ + jnp.where(dz == 0, 0, jnp.where(dz <= 4, 2 * dz - 1, 16 - 2 * dz))
-    return table, place
+    order = jnp.arange(own.shape[0], dtype=jnp.int32)
+    slot_of = jnp.max(jnp.where(place[None, :] == views[:, None], order[None, :], 0), axis=1)
+    return table, place, slot_of
 
 
 def body(query_rows, key_rows, value_rows, out_weight, out_grad, source_view, source_block):
-    tokens, columns = query_rows.shape
-    head = lax.axis_index("head")
-    table, place = routes(source_view, source_block)
-    cut = (NB, BLOCK, columns)
-    got_k, got_v, og = fetch(table, out_grad, key_rows.reshape(cut), value_rows.reshape(cut))
-    flat = (NY * NZ, BLOCK, columns)
-    w_rows = lax.dynamic_slice_in_dim(out_weight, head * columns, columns, 0)
-    w_cols = lax.dynamic_slice_in_dim(out_weight, head * columns, columns, 1)
-    att, dq, ck, cv = attention(
-        place, query_rows, got_k.reshape(flat), got_v.reshape(flat), og, w_rows
+    cut = (NB, BLOCK, COLS)
+    table, place, slot_of = routes(source_view, source_block)
+    mixed, dq, kg, vg = layer(
+        table, place, slot_of,
+        query_rows, key_rows.reshape(cut), value_rows.reshape(cut), out_weight, out_grad,
     )
-    mixed, kg, vg = give_back(table, att, w_cols, ck.reshape(got_k.shape), cv.reshape(got_v.shape))
-    return mixed, dq, kg.reshape(tokens, columns), vg.reshape(tokens, columns)
+    return mixed, dq, kg.reshape(query_rows.shape), vg.reshape(query_rows.shape)
 
 
 def solution(mesh):

time: 137 us -> 116 us (0.85)
  Pallas kernels: 126 us -> 104 us
  other arithmetic: 0.25 us -> 2.26 us
    pallas_call x3 -> x1, Pallas kernels: 126 us -> 104 us  [layer(): pl.pallas_call(layer_kernel, out_shape=(rows, rows, cut, cut), in_specs=[...]
    add x1 -> x2, other arithmetic: 0.02 us -> 1.44 us  [routes(): dy * NZ + jnp.where(dz == 0, 0, jnp.where(dz <= 4, 2 * dz - 1, 16 - 2 * dz))]
    unnamed x15 -> x6, local copies, waits for them, and re-layouts: 7.98 us -> 8.22 us
where the time goes in v3:
time: 116 us
  Pallas kernels  104 us (90%)
  local copies, waits for them, and re-layouts  8.88 us (8%)
  other arithmetic  2.26 us (2%)
    pallas_call x1, Pallas kernels, layer(): pl.pallas_call(layer_kernel, out_shape=(rows, rows, cut, cut), in_specs=[...  104 us
    unnamed x6, local copies, waits for them, and re-layouts  8.22 us

profile of v3, /device:TPU:2, one launch (start us, length us, event | category | flops | bytes accessed | tf_op | source)
XLA Modules:
  0.0 115.9 jit_solution(7289604031271095168)
XLA Ops:
  0.6 0.9 fusion.3
  1.5 0.5 fusion.8.place
  2.1 0.6 select_reduce_fusion.1.slot_of
  2.7 0.8 copy.16
  3.5 0.8 copy.15
  4.2 0.2 select_reduce_fusion
  4.5 0.7 reshape.25.table
  5.1 104.1 %layer.1 = (bf16[1024,128]{1,0:T(8,128)(2,1)}, bf16[1024,128]{1,0:T(8,128)(2,1)}, bf16[8,128,128]{2,1,0:T(8,128)(2,1)}, bf16[8,128,128]{2,1,0:T(8,128)(2,1)}) custom-call(s32[1024]{0:T(1024)} %reshape.25.table, s32[16]{0:T(128)} %fusion.8.place, s32[32]{0:T(128)} %select_reduce_fusion.1.slot_of, bf16[1024,128]{1,0:T(8,128)(2,1)} %q_hbm.1, ...), custom_call_target="tpu_custom_call" | custom-call | tf_op jit(solution)/shard_map/layer/pallas_call | solution.py:648
  109.2 1.7 %copy.21 = bf16[1024,128]{1,0:T(8,128)(2,1)} copy(bf16[1024,128]{1,0:T(8,128)(2,1)} %get-tuple-element.18) | data formatting | bytes 524288
  110.9 1.7 %copy.22 = bf16[1024,128]{1,0:T(8,128)(2,1)} copy(bf16[1024,128]{1,0:T(8,128)(2,1)} %get-tuple-element.19) | data formatting | bytes 524288
  112.6 1.7 %copy.23 = bf16[1024,128]{1,0:T(8,128)(2,1)} copy(bf16[1024,128]{1,0:T(8,128)(2,1)} %bitcast.7) | data formatting | bytes 524288
  114.2 1.7 %copy.24 = bf16[1024,128]{1,0:T(8,128)(2,1)} copy(bf16[1024,128]{1,0:T(8,128)(2,1)} %bitcast.6) | data formatting | bytes 524288

commit v4 on v3

--- a/solution.py
+++ b/solution.py
@@ -70,11 +70,11 @@
 
     def pick(self, table, dz, k, sz):
         taker = self.zplus(dz) * NY + self.yplus(k)
-        return table[taker * (NZ * NY) + self.zplus(sz) * NY + self.y]
+        return table[self.zplus(sz) * NY + self.y, taker]
 
     def pick_abs(self, table, dz, yd, sz):
         taker = self.zplus(dz) * NY + yd
-        return table[taker * (NZ * NY) + self.zplus(sz) * NY + self.y]
+        return table[self.zplus(sz) * NY + self.y, taker]
 
 
 def greet(here, zy=True, x=True):
@@ -260,7 +260,7 @@
                     copy.wait_send()
 
 
-RETURN_PIECES = ((5, 8), (3, 5), (1, 3), (0, 1))
+RETURN_PIECES = ((7, 8), (5, 7), (3, 5), (1, 3), (0, 1))
 
 
 class Return:
@@ -330,20 +330,21 @@
     def step(self, n):
         here, table = self.here, self.table
         h = NB // 2
-        if n == 0:
-            for piece in range(4):
-                self.start_y(piece)
         if n == 1:
             self.wait_y(0)
-            for copy in self.c4 + self.c3[:2]:
+            for copy in self.c4:
                 copy.start()
         if n == 2:
+            self.wait_y(1)
+            for copy in self.c3[:2]:
+                copy.start()
+        if n == 3:
             for copy in self.c4:
                 copy.wait_recv()
             for copy in self.c3[2:]:
                 copy.start()
-        if n == 3:
-            self.wait_y(1)
+        if n == 4:
+            self.wait_y(2)
             for copy in self.c3:
                 copy.wait_recv()
             for part in range(2):
@@ -358,10 +359,10 @@
                         self.out2[s, b] = self.total(b, [], terms)
                 for s in range(2):
                     self.c2[part * 2 + s].start()
-        if n in (4, 5):
-            part = n - 4
-            if n == 4:
-                self.wait_y(2)
+        if n in (5, 6):
+            part = n - 5
+            if n == 5:
+                self.wait_y(3)
             for s, d in ((0, 1), (1, -1)):
                 self.c2[part * 2 + s].wait_recv()
                 terms = self.here_terms(1 + s, -d)
@@ -369,16 +370,16 @@
                     self.out1[s, b] = self.total(b, [self.two[s, b]], terms)
             for s in range(2):
                 self.c1[part * 2 + s].start()
-        if n in (6, 7):
-            part = n - 6
-            if n == 6:
-                self.wait_y(3)
+        if n in (7, 8):
+            part = n - 7
+            if n == 7:
+                self.wait_y(4)
             for s in range(2):
                 self.c1[part * 2 + s].wait_recv()
             terms = self.here_terms(0, 0)
             for b in range(part * h, part * h + h):
                 self.out[b] = self.total(b, [self.one[0, b], self.one[1, b]], terms)
-        if n == 8:
+        if n == 9:
             for copy in self.c4 + self.c3 + self.c2 + self.c1:
                 copy.wait_send()
             for piece in self.cy:
@@ -390,10 +391,32 @@
     return pl.ds(pl.multiple_of(i * size, size), size)
 
 
+def routes(view, sv_ref, sb_ref, pack_ref):
+    slots, views = sv_ref.shape
+    sv, sb = sv_ref[...], sb_ref[...]
+    wide = (views, views)
+    source = lax.broadcasted_iota(jnp.int32, wide, 0)
+    table = jnp.full(wide, -1, jnp.int32)
+    for j in range(slots):
+        same = jnp.broadcast_to(sv[j : j + 1, :], wide) == source
+        table = jnp.where(same, jnp.broadcast_to(sb[j : j + 1, :], wide), table)
+    pack_ref[0:views, 0:views] = table
+    lanes = lax.broadcasted_iota(jnp.int32, sv.shape, 1)
+    own = jnp.sum(jnp.where(lanes == view, sv, 0), axis=1, keepdims=True)
+    dz = (view // NY - own // NY + NZ) & (NZ - 1)
+    dy = ((view & (NY - 1)) - (own & (NY - 1)) + NY) & (NY - 1)
+    near = jnp.where(dz == 0, 0, jnp.where(dz <= NZ // 2, 2 * dz - 1, 2 * NZ - 2 * dz))
+    place = jnp.broadcast_to(dy * NZ + near, (slots, BLOCK))
+    pack_ref[views : views + slots, :] = place
+    order = lax.broadcasted_iota(jnp.int32, place.shape, 0)
+    spot = lax.broadcasted_iota(jnp.int32, place.shape, 1)
+    slot_of = jnp.max(jnp.where(place == spot, order, 0), axis=0, keepdims=True)
+    pack_ref[views + slots : views + slots + 8, :] = jnp.broadcast_to(slot_of, (8, BLOCK))
+
+
 def layer_kernel(
-    table, place, slot_of,
-    q_hbm, k_hbm, v_hbm, w_hbm, og_hbm,
-    mixed_hbm, dq_hbm, ok_hbm, ov_hbm,
+    sv_ref, sb_ref, q_hbm, k_hbm, v_hbm, w_hbm, og_hbm,
+    mixed_ref, dq_ref, ok_ref, ov_ref,
     *scratch,
 ):
     fbk, fbv, rbk, rbv = scratch[:6], scratch[6:12], scratch[12:18], scratch[18:24]
@@ -401,12 +424,12 @@
         k_own, v_own, og_own, q_s, w_rows, w_cols,
         got_k, got_v, og_all, at_all, sent_k, sent_v, held_k, held_v,
         qm, qtm, dam, datm, k_s, kt_s, v_s, vt_s, s_s, p_s,
-        att_t, dq_t, grad_s, att_s, dq_s, mixed_s, ok_s, ov_s,
+        att_t, dq_t, grad_s, att_s, inv_s, delta_s, pack_v, pack,
         send, recv, local,
     ) = scratch[24:]
     here = Place()
     copies = Copies(send, recv)
-    slots = place.shape[0]
+    slots, views = sv_ref.shape
     keys = slots * BLOCK
     tokens = q_s.shape[0]
     chunks = keys // KC
@@ -425,21 +448,18 @@
             )
         )
     ]
-    stores = [
-        pltpu.make_async_copy(src, dst, local.at[len(loads) + i])
-        for i, (src, dst) in enumerate(
-            ((dq_s, dq_hbm), (mixed_s, mixed_hbm), (ov_s, ov_hbm), (ok_s, ok_hbm))
-        )
-    ]
     for load in loads:
         load.start()
+    tables = pltpu.make_async_copy(pack_v, pack, local.at[len(loads)])
+    routes(here.view, sv_ref, sb_ref, pack_v)
+    tables.start()
 
     og = Gather(here, copies, og_own, og_all)
-    fk = Fetch(here, copies, table, k_own, got_k, fbk)
-    fv = Fetch(here, copies, table, v_own, got_v, fbv)
+    fk = Fetch(here, copies, pack, k_own, got_k, fbk)
+    fv = Fetch(here, copies, pack, v_own, got_v, fbv)
     at = Gather(here, copies, att_s, at_all)
-    rk = Return(here, copies, table, sent_k, held_k, ok_s, rbk)
-    rv = Return(here, copies, table, sent_v, held_v, ov_s, rbv)
+    rk = Return(here, copies, pack, sent_k, held_k, ok_ref, rbk)
+    rv = Return(here, copies, pack, sent_v, held_v, ov_ref, rbv)
 
     greet(here)
     loads[0].wait()
@@ -447,6 +467,7 @@
     fk.offer(1)
     loads[1].wait()
     og.step(0)
+    tables.wait()
     fk.step(0)
     loads[2].wait()
     fv.step(0)
@@ -493,18 +514,14 @@
     fv.step(2)
     fk.step(6)
     for j in range(slots):
-        rows = pl.ds(j * BLOCK, BLOCK)
-        block = got_k[place[j]]
-        k_s[rows, :] = block
-        kt_s[:, rows] = block.T
+        k_s[pl.ds(j * BLOCK, BLOCK), :] = got_k[pack[views + j, 0]]
 
     steps = 2 * (tokens // QB)
 
     def forward(i, carry):
-        for n, at_step in ((3, 2), (4, 6), (5, 7)):
-            @pl.when(i == at_step)
-            def _():
-                fv.step(n)
+        @pl.when(i == 2)
+        def _():
+            fv.step(3)
 
         h = lax.rem(i, 2)
         cols = rows_at(i // 2, QB)
@@ -521,88 +538,122 @@
         for c in range(chunks):
             rows = pl.ds(c * KC, KC)
             e = jnp.exp2(s_s[rows, :] * (SCALE * LOG2E) - shift)
-            s_s[rows, :] = e
+            p_s[h, rows, cols] = e.astype(BF)
             total = total + jnp.sum(e, axis=0, keepdims=True)
-        inv = 1.0 / total
-        for c in range(chunks):
-            rows = pl.ds(c * KC, KC)
-            p_s[h, rows, cols] = (s_s[rows, :] * inv).astype(BF)
+        inv = jnp.broadcast_to(1.0 / total, (8, QB))
+        inv_s[h, :, cols] = inv
+        down = inv.T[:, 0:1]
+        dam[h, cols, :] = (dam[h, cols, :].astype(F32) * down).astype(BF)
+        qm[h, cols, :] = (qm[h, cols, :].astype(F32) * down).astype(BF)
         return carry
 
     lax.fori_loop(0, steps, forward, 0)
 
-    def contract(scale, right):
-        def one(c, carry):
-            rows = rows_at(c, KC)
-            g = dot(p_s[0, rows, :], right[0]) + dot(p_s[1, rows, :], right[1])
-            if scale is not None:
-                g = g * scale
-            g = g.astype(BF)
-            for b in range(KC // BLOCK):
-                grad_s[c * (KC // BLOCK) + b] = g[b * BLOCK : (b + 1) * BLOCK, :]
-            return carry
-
-        lax.fori_loop(0, chunks, one, 0)
+    def grads(c, rows, right, scale):
+        g = dot(p_s[0, rows, :], right[0]) + dot(p_s[1, rows, :], right[1])
+        if scale is not None:
+            g = g * scale
+        g = g.astype(BF)
+        for b in range(KC // BLOCK):
+            grad_s[c * (KC // BLOCK) + b] = g[b * BLOCK : (b + 1) * BLOCK, :]
+
+    def value_grads(c, carry):
+        grads(c, rows_at(c, KC), dam, None)
+        return carry
 
     def hand_out(sent, held):
         for e in range(NZ):
-            held[0, e] = grad_s[slot_of[e]]
+            held[0, e] = grad_s[pack[views + slots, e]]
         for k in range(1, NY):
             for e in range(NZ):
-                sent[k - 1, e] = grad_s[slot_of[k * NZ + e]]
-
-    contract(None, dam)
+                sent[k - 1, e] = grad_s[pack[views + slots, k * NZ + e]]
+
+    lax.fori_loop(0, chunks, value_grads, 0)
+    fv.step(4)
     hand_out(sent_v, held_v)
-    rv.step(0)
+    rv.start_y(0)
+    fv.step(5)
+    rv.start_y(1)
+    rv.step(1)
     fv.step(6)
+    rv.start_y(2)
+    rv.start_y(3)
+    rv.start_y(4)
     for j in range(slots):
         rows = pl.ds(j * BLOCK, BLOCK)
-        block = got_v[place[j]]
+        block = got_v[pack[views + j, 0]]
         v_s[rows, :] = block
         vt_s[:, rows] = block.T
 
-    def backward(i, carry):
-        for n, at_step in ((1, 3), (2, 5)):
-            @pl.when(i == at_step)
-            def _():
-                rv.step(n)
-
+    def attend(i, carry):
         h = lax.rem(i, 2)
         cols = rows_at(i // 2, QB)
         band = rows_at(h, HEAD_DIM)
-        att = dot(vt_s[band, :], p_s[h, :, cols]).astype(BF)
+        att = dot(vt_s[band, :], p_s[h, :, cols]) * inv_s[h, 0:1, cols]
+        att = att.astype(BF)
         att_t[band, cols] = att
         delta = jnp.sum(
             att.astype(F32) * datm[h, band, cols].astype(F32), axis=0, keepdims=True
         )
-        dat = datm[h, :, cols]
-        for c in range(chunks):
-            rows = pl.ds(c * KC, KC)
-            dp = dot(v_s[rows, :], dat)
-            p_s[h, rows, cols] = (p_s[h, rows, cols].astype(F32) * (dp - delta)).astype(BF)
-        dq_t[band, cols] = (dot(kt_s[band, :], p_s[h, :, cols]) * SCALE).astype(BF)
+        delta_s[h, :, cols] = jnp.broadcast_to(delta, (8, QB))
         return carry
 
-    lax.fori_loop(0, steps, backward, 0)
+    lax.fori_loop(0, steps, attend, 0)
     att_s[...] = att_t[...].T
-    dq_s[...] = dq_t[...].T
-    stores[0].start()
     at.step(0)
-    contract(SCALE, qm)
+
+    def key_grads(c, carry):
+        @pl.when(c == 1)
+        def _():
+            rv.step(2)
+            rv.step(3)
+
+        @pl.when(c == 6)
+        def _():
+            at.step(1)
+
+        rows = rows_at(c, KC)
+        right = v_s[rows, :]
+        for h in range(2):
+            for i in range(tokens // QB):
+                cols = pl.ds(i * QB, QB)
+                dp = dot(right, datm[h, :, cols]) - delta_s[h, 0:1, cols]
+                p_s[h, rows, cols] = (p_s[h, rows, cols].astype(F32) * dp).astype(BF)
+        grads(c, rows, qm, SCALE)
+        return carry
+
+    lax.fori_loop(0, chunks, key_grads, 0)
     hand_out(sent_k, held_k)
-    rk.step(0)
-    rv.step(3)
-    at.step(1)
-    rk.step(1)
+    rk.start_y(0)
+    rk.start_y(1)
     rv.step(4)
+    rk.start_y(2)
+    rk.start_y(3)
+    rk.start_y(4)
+    for j in range(slots):
+        kt_s[:, pl.ds(j * BLOCK, BLOCK)] = k_s[pl.ds(j * BLOCK, BLOCK), :].T
+
+    def query_grads(i, carry):
+        @pl.when(i == 4)
+        def _():
+            rk.step(1)
+
+        h = lax.rem(i, 2)
+        cols = rows_at(i // 2, QB)
+        band = rows_at(h, HEAD_DIM)
+        dq = dot(kt_s[band, :], p_s[h, :, cols]) * (inv_s[h, 0:1, cols] * SCALE)
+        dq_t[band, cols] = dq.astype(BF)
+        return carry
+
+    lax.fori_loop(0, steps, query_grads, 0)
+    rk.step(2)
     rv.step(5)
-    rk.step(2)
     at.step(2)
+    rk.step(3)
+    rv.step(6)
+    dq_ref[...] = dq_t[...].T
+    rk.step(4)
     loads[5].wait()
-    rv.step(6)
-    rv.step(7)
-    stores[2].start()
-    rk.step(3)
     at.step(3)
 
     def mix(i, carry):
@@ -611,31 +662,30 @@
         for g in range(2 * NX):
             part = dot(at_all[g, rows, :], w_cols[pl.ds(g * COLS, COLS), :])
             acc = part if acc is None else acc + part
-        mixed_s[rows, :] = acc.astype(BF)
+        mixed_ref[rows, :] = acc.astype(BF)
         return carry
 
+    rk.step(5)
+    rv.step(7)
+    rv.step(8)
+    rk.step(6)
     lax.fori_loop(0, tokens // QB, mix, 0)
-    stores[1].start()
-    rk.step(4)
-    rk.step(5)
     fk.step(7)
     fv.step(7)
     og.step(4)
     at.step(4)
-    rv.step(8)
-    rk.step(6)
+    rv.step(9)
     rk.step(7)
-    stores[3].start()
     rk.step(8)
-    for store in stores:
-        store.wait()
-
-
-def layer(table, place, slot_of, q, k, v, w, og):
+    rk.step(9)
+
+
+def layer(sv, sb, q, k, v, w, og):
     tokens = q.shape[0]
-    keys = place.shape[0] * BLOCK
+    slots, views = sv.shape
+    keys = slots * BLOCK
     hbm = pl.BlockSpec(memory_space=pl.ANY)
-    smem = pl.BlockSpec(memory_space=pltpu.SMEM)
+    vm = pl.BlockSpec(memory_space=pltpu.VMEM)
 
     def vmem(*shape, dtype=BF):
         return pltpu.VMEM(shape, dtype)
@@ -648,8 +698,8 @@
     return pl.pallas_call(
         layer_kernel,
         out_shape=(rows, rows, cut, cut),
-        in_specs=[smem, smem, smem] + [hbm] * 5,
-        out_specs=(hbm,) * 4,
+        in_specs=[vm, vm] + [hbm] * 5,
+        out_specs=(vm,) * 4,
         scratch_shapes=bufs(Fetch) + bufs(Fetch) + bufs(Return) + bufs(Return) + [
             vmem(NB, BLOCK, COLS),
             vmem(NB, BLOCK, COLS),
@@ -677,44 +727,52 @@
             vmem(2, keys, tokens),
             vmem(COLS, tokens),
             vmem(COLS, tokens),
-            vmem(keys // BLOCK, BLOCK, COLS),
+            vmem(slots, BLOCK, COLS),
             vmem(tokens, COLS),
-            vmem(tokens, COLS),
-            vmem(tokens, COLS),
-            vmem(NB, BLOCK, COLS),
-            vmem(NB, BLOCK, COLS),
+            vmem(2, 8, tokens, dtype=F32),
+            vmem(2, 8, tokens, dtype=F32),
+            vmem(views + slots + 8, BLOCK, dtype=jnp.int32),
+            pltpu.SMEM((views + slots + 8, BLOCK), jnp.int32),
             pltpu.SemaphoreType.DMA((136,)),
             pltpu.SemaphoreType.DMA((136,)),
-            pltpu.SemaphoreType.DMA((10,)),
+            pltpu.SemaphoreType.DMA((8,)),
         ],
         compiler_params=pltpu.CompilerParams(
             collective_id=0, has_side_effects=True, vmem_limit_bytes=56 * 2**20
         ),
         name="layer",
-    )(table, place, slot_of, q, k, v, w, og)
-
-
-def routes(source_view, source_block):
-    view = lax.axis_index("view")
-    views = jnp.arange(NZ * NY, dtype=jnp.int32)
-    same = source_view[:, :, None] == views[None, None, :]
-    table = jnp.max(jnp.where(same, source_block[:, :, None], -1), axis=1).reshape(-1)
-    own = lax.dynamic_index_in_dim(source_view, view, 0, keepdims=False)
-    dz = lax.rem(view // NY - own // NY + NZ, NZ)
-    dy = lax.rem(lax.rem(view, NY) - lax.rem(own, NY) + NY, NY)
-    place = dy * NZ + jnp.where(dz == 0, 0, jnp.where(dz <= 4, 2 * dz - 1, 16 - 2 * dz))
-    order = jnp.arange(own.shape[0], dtype=jnp.int32)
-    slot_of = jnp.max(jnp.where(place[None, :] == views[:, None], order[None, :], 0), axis=1)
-    return table, place, slot_of
+    )(sv, sb, q, k, v, w, og)
+
+
+def finish_kernel(*refs):
+    sems = refs[-1]
+    n = (len(refs) - 1) // 2
+    moves = [pltpu.make_async_copy(refs[i], refs[n + i], sems.at[i]) for i in range(n)]
+    for move in moves:
+        move.start()
+    for move in moves:
+        move.wait()
+
+
+def finish(*arrays):
+    vm = pl.BlockSpec(memory_space=pltpu.VMEM)
+    hbm = pl.BlockSpec(memory_space=pl.ANY)
+    return pl.pallas_call(
+        finish_kernel,
+        out_shape=tuple(jax.ShapeDtypeStruct(a.shape, a.dtype) for a in arrays),
+        in_specs=[vm] * len(arrays),
+        out_specs=(hbm,) * len(arrays),
+        scratch_shapes=[pltpu.SemaphoreType.DMA((len(arrays),))],
+        name="finish",
+    )(*arrays)
 
 
 def body(query_rows, key_rows, value_rows, out_weight, out_grad, source_view, source_block):
     cut = (NB, BLOCK, COLS)
-    table, place, slot_of = routes(source_view, source_block)
-    mixed, dq, kg, vg = layer(
-        table, place, slot_of,
+    mixed, dq, kg, vg = finish(*layer(
+        source_view.T, source_block.T,
         query_rows, key_rows.reshape(cut), value_rows.reshape(cut), out_weight, out_grad,
-    )
+    ))
     return mixed, dq, kg.reshape(query_rows.shape), vg.reshape(query_rows.shape)
 
 

time: 116 us -> 107 us (0.922)
  local copies, waits for them, and re-layouts: 8.88 us -> 0 us
  Pallas kernels: 104 us -> 107 us
  other arithmetic: 2.26 us -> 0 us
    unnamed x6 -> x0, local copies, waits for them, and re-layouts: 8.22 us -> none
    pallas_call x0 -> x1, Pallas kernels: none -> 2.18 us  [finish(): pl.pallas_call(finish_kernel, out_shape=tuple((jax.ShapeDtypeStruct(a.sha...]
    add x2 -> x0, other arithmetic: 1.44 us -> none  [routes(): dy * NZ + jnp.where(dz == 0, 0, jnp.where(dz <= 4, 2 * dz - 1, 16 - 2 * dz))]
where the time goes in v4:
time: 107 us
  Pallas kernels  107 us (100%)
    pallas_call x1, Pallas kernels, layer(): pl.pallas_call(layer_kernel, out_shape=(rows, rows, cut, cut), in_specs=[...  104 us
    pallas_call x1, Pallas kernels, finish(): pl.pallas_call(finish_kernel, out_shape=tuple((jax.ShapeDtypeStruct(a.sha...  2.18 us

profile of v4, /device:TPU:2, one launch (start us, length us, event | category | flops | bytes accessed | tf_op | source)
XLA Modules:
  0.0 107.3 jit_solution(976045436335385062)
XLA Ops:
  0.6 104.5 %layer.1 = (bf16[1024,128]{1,0:T(8,128)(2,1)}, bf16[1024,128]{1,0:T(8,128)(2,1)}, bf16[8,128,128]{2,1,0:T(8,128)(2,1)}, bf16[8,128,128]{2,1,0:T(8,128)(2,1)}) custom-call(s32[16,32]{1,0:T(8,128)} %bitcast.8, s32[16,32]{1,0:T(8,128)} %bitcast.9, bf16[1024,128]{1,0:T(8,128)(2,1)} %q_hbm.1, bf16[8,128,128]{2,1,0:T(8,128)(2,1)} %bitcast.6, ...), custom_call_target="tpu_custom_call" | custom-call | tf_op jit(solution)/shard_map/layer/pallas_call | solution.py:698
  105.1 2.2 %finish.1 = (bf16[1024,128]{1,0:T(8,128)(2,1)}, bf16[1024,128]{1,0:T(8,128)(2,1)}, bf16[8,128,128]{2,1,0:T(8,128)(2,1)}, bf16[8,128,128]{2,1,0:T(8,128)(2,1)}) custom-call(bf16[1024,128]{1,0:T(8,128)(2,1)} %get-tuple-element.12.refs_0_, bf16[1024,128]{1,0:T(8,128)(2,1)} %get-tuple-element.13.refs_1_, bf16[8,128,128]{2,1,0:T(8,128)(2,1)} %get-tuple-element.14.refs_2_, ...), custom_call_target="tpu_custom_call" | custom-call | tf_op jit(solution)/shard_map/finish/pallas_call | solution.py:760

commit v5 on v4

--- a/solution.py
+++ b/solution.py
@@ -77,16 +77,13 @@
         return table[self.zplus(sz) * NY + self.y, taker]
 
 
-def greet(here, zy=True, x=True):
+def greet(here):
     barrier = pltpu.get_barrier_semaphore()
-    peers = []
-    if zy:
-        peers += [here.at_z(1), here.at_z(-1), here.at_y(1), here.at_y(2), here.at_y(3)]
-    if x:
-        peers += [here.at_x(1), here.at_x(-1), here.partner()]
+    peers = [here.at_z(1), here.at_z(-1), here.at_y(1), here.at_y(2), here.at_y(3)]
+    peers += [here.at_x(1), here.at_x(-1), here.partner()]
     for peer in peers:
         pl.semaphore_signal(barrier, inc=1, device_id=peer, device_id_type=MESH)
-    pl.semaphore_wait(barrier, len(peers))
+    return lambda: pl.semaphore_wait(barrier, len(peers))
 
 
 class Gather:
@@ -164,8 +161,9 @@
                 self.c2.append(
                     mk(one.at[s, pl.ds(part * h, h)], two.at[s, pl.ds(part * h, h)], way)
                 )
-        for s, way in enumerate(ways):
-            self.c3.append(mk(fwd.at[s], three.at[s], way))
+        for a, size in ((4, 2), (0, 4)):
+            for s, way in enumerate(ways):
+                self.c3.append(mk(fwd.at[s, pl.ds(a, size)], three.at[s, pl.ds(a, size)], way))
         for s, way in enumerate(ways):
             self.c4.append(mk(three.at[s, pl.ds(4, 2)], four.at[s], way))
         self.cy = []
@@ -235,12 +233,15 @@
             for s in range(2):
                 self.c3[s].wait_recv()
                 self.c4[s].start()
+        if n == 5:
+            for copy in self.c3[2:]:
+                copy.wait_recv()
             for k in range(NY):
                 yd = here.yplus(k)
                 self.put(k, 5, self.three[0, yd])
                 self.put(k, 6, self.three[1, yd])
             self.start_y(3)
-        if n == 5:
+        if n == 6:
             for copy in self.c4:
                 copy.wait_recv()
             for k in range(NY):
@@ -248,11 +249,11 @@
                 low = lax.rem(yd, 2)
                 self.put(k, 7, jnp.where(yd < 2, self.four[0, low], self.four[1, low]))
             self.start_y(4)
-        if n == 6:
+        if n == 7:
             for piece in self.cy:
                 for copy in piece:
                     copy.wait_recv()
-        if n == 7:
+        if n == 8:
             for copy in self.c1 + self.c2 + self.c3 + self.c4:
                 copy.wait_send()
             for piece in self.cy:
@@ -343,25 +344,26 @@
                 copy.wait_recv()
             for copy in self.c3[2:]:
                 copy.start()
-        if n == 4:
-            self.wait_y(2)
-            for copy in self.c3:
-                copy.wait_recv()
-            for part in range(2):
-                for s, d in ((0, 1), (1, -1)):
-                    terms = self.here_terms(3 + s, -2 * d)
-                    for k in range(4):
-                        terms.append((here.pick(table, d, k, -2 * d), self.three.at[s, k]))
-                    for i in range(2):
-                        pick = here.pick_abs(table, 2 * d, 2 * s + i, -2 * d)
-                        terms.append((pick, self.three.at[s, 4 + i]))
-                    for b in range(part * h, part * h + h):
-                        self.out2[s, b] = self.total(b, [], terms)
-                for s in range(2):
-                    self.c2[part * 2 + s].start()
-        if n in (5, 6):
-            part = n - 5
-            if n == 5:
+        if n in (4, 5):
+            part = n - 4
+            if n == 4:
+                self.wait_y(2)
+                for copy in self.c3:
+                    copy.wait_recv()
+            for s, d in ((0, 1), (1, -1)):
+                terms = self.here_terms(3 + s, -2 * d)
+                for k in range(4):
+                    terms.append((here.pick(table, d, k, -2 * d), self.three.at[s, k]))
+                for i in range(2):
+                    pick = here.pick_abs(table, 2 * d, 2 * s + i, -2 * d)
+                    terms.append((pick, self.three.at[s, 4 + i]))
+                for b in range(part * h, part * h + h):
+                    self.out2[s, b] = self.total(b, [], terms)
+            for s in range(2):
+                self.c2[part * 2 + s].start()
+        if n in (6, 7):
+            part = n - 6
+            if n == 6:
                 self.wait_y(3)
             for s, d in ((0, 1), (1, -1)):
                 self.c2[part * 2 + s].wait_recv()
@@ -370,16 +372,16 @@
                     self.out1[s, b] = self.total(b, [self.two[s, b]], terms)
             for s in range(2):
                 self.c1[part * 2 + s].start()
-        if n in (7, 8):
-            part = n - 7
-            if n == 7:
+        if n in (8, 9):
+            part = n - 8
+            if n == 8:
                 self.wait_y(4)
             for s in range(2):
                 self.c1[part * 2 + s].wait_recv()
             terms = self.here_terms(0, 0)
             for b in range(part * h, part * h + h):
                 self.out[b] = self.total(b, [self.one[0, b], self.one[1, b]], terms)
-        if n == 9:
+        if n == 10:
             for copy in self.c4 + self.c3 + self.c2 + self.c1:
                 copy.wait_send()
             for piece in self.cy:
@@ -403,20 +405,26 @@
     pack_ref[0:views, 0:views] = table
     lanes = lax.broadcasted_iota(jnp.int32, sv.shape, 1)
     own = jnp.sum(jnp.where(lanes == view, sv, 0), axis=1, keepdims=True)
+    own = jnp.broadcast_to(own, (slots, BLOCK))
     dz = (view // NY - own // NY + NZ) & (NZ - 1)
     dy = ((view & (NY - 1)) - (own & (NY - 1)) + NY) & (NY - 1)
     near = jnp.where(dz == 0, 0, jnp.where(dz <= NZ // 2, 2 * dz - 1, 2 * NZ - 2 * dz))
-    place = jnp.broadcast_to(dy * NZ + near, (slots, BLOCK))
-    pack_ref[views : views + slots, :] = place
-    order = lax.broadcasted_iota(jnp.int32, place.shape, 0)
-    spot = lax.broadcasted_iota(jnp.int32, place.shape, 1)
-    slot_of = jnp.max(jnp.where(place == spot, order, 0), axis=0, keepdims=True)
-    pack_ref[views + slots : views + slots + 8, :] = jnp.broadcast_to(slot_of, (8, BLOCK))
+    place = dy * NZ + near
+    turn = (NZ - 1 - near) * NY + dy
+    lane = lax.broadcasted_iota(jnp.int32, place.shape, 1)
+    taken = jnp.max(jnp.where(turn == lane, 1, 0), axis=0, keepdims=True)
+    taken = jnp.broadcast_to(taken, place.shape)
+    rank = jnp.sum(jnp.where(lane < turn, taken, 0), axis=1, keepdims=True)
+    rank = jnp.broadcast_to(rank, place.shape)
+    place_of = jnp.max(jnp.where(rank == lane, place, 0), axis=0, keepdims=True)
+    rank_of = jnp.max(jnp.where(place == lane, rank, 0), axis=0, keepdims=True)
+    pack_ref[views : views + 8, :] = jnp.broadcast_to(place_of, (8, BLOCK))
+    pack_ref[views + 8 : views + 16, :] = jnp.broadcast_to(rank_of, (8, BLOCK))
 
 
 def layer_kernel(
     sv_ref, sb_ref, q_hbm, k_hbm, v_hbm, w_hbm, og_hbm,
-    mixed_ref, dq_ref, ok_ref, ov_ref,
+    mixed_hbm, dq_hbm, ok_hbm, ov_hbm,
     *scratch,
 ):
     fbk, fbv, rbk, rbv = scratch[:6], scratch[6:12], scratch[12:18], scratch[18:24]
@@ -424,7 +432,7 @@
         k_own, v_own, og_own, q_s, w_rows, w_cols,
         got_k, got_v, og_all, at_all, sent_k, sent_v, held_k, held_v,
         qm, qtm, dam, datm, k_s, kt_s, v_s, vt_s, s_s, p_s,
-        att_t, dq_t, grad_s, att_s, inv_s, delta_s, pack_v, pack,
+        att_t, dq_t, grad_s, att_s, mixed_ref, dq_ref, ok_ref, ov_ref, inv_s, delta_s, pack_v, pack,
         send, recv, local,
     ) = scratch[24:]
     here = Place()
@@ -450,6 +458,19 @@
     ]
     for load in loads:
         load.start()
+    stores = [
+        pltpu.make_async_copy(src, dst, local.at[len(loads) + 1 + i])
+        for i, (src, dst) in enumerate(
+            (
+                (dq_ref, dq_hbm),
+                (mixed_ref, mixed_hbm),
+                (ov_ref, ov_hbm),
+                (ok_ref.at[pl.ds(0, NB // 2)], ok_hbm.at[pl.ds(0, NB // 2)]),
+                (ok_ref.at[pl.ds(NB // 2, NB // 2)], ok_hbm.at[pl.ds(NB // 2, NB // 2)]),
+            )
+        )
+    ]
+    arrived = greet(here)
     tables = pltpu.make_async_copy(pack_v, pack, local.at[len(loads)])
     routes(here.view, sv_ref, sb_ref, pack_v)
     tables.start()
@@ -461,7 +482,7 @@
     rk = Return(here, copies, pack, sent_k, held_k, ok_ref, rbk)
     rv = Return(here, copies, pack, sent_v, held_v, ov_ref, rbv)
 
-    greet(here)
+    arrived()
     loads[0].wait()
     fk.offer(0)
     fk.offer(1)
@@ -483,7 +504,6 @@
     fv.offer(0)
     og.step(1)
     fk.step(3)
-    fv.offer(1)
     og.step(2)
     loads[4].wait()
     og.step(3)
@@ -509,35 +529,34 @@
 
     lax.fori_loop(0, tokens // QB, project, 0)
     fk.step(4)
+    fv.offer(1)
+    fk.step(5)
     fv.step(1)
-    fk.step(5)
+    fk.step(6)
     fv.step(2)
-    fk.step(6)
+    fk.step(7)
     for j in range(slots):
-        k_s[pl.ds(j * BLOCK, BLOCK), :] = got_k[pack[views + j, 0]]
-
-    steps = 2 * (tokens // QB)
-
-    def forward(i, carry):
-        @pl.when(i == 2)
-        def _():
-            fv.step(3)
-
-        h = lax.rem(i, 2)
-        cols = rows_at(i // 2, QB)
-        qt = qtm[h, :, cols]
-        top = None
+        k_s[pl.ds(j * BLOCK, BLOCK), :] = got_k[pack[views, j]]
+
+    tiles = tokens // QB
+    turns = SCALE * LOG2E
+
+    def score(h, cols, c, top):
+        rows = pl.ds(c * KC, KC)
+        s = dot(k_s[rows, :], qtm[h, :, cols])
+        s_s[h, rows, :] = s
+        return jnp.maximum(top, jnp.max(s, axis=0, keepdims=True))
+
+    lowest = jnp.full((1, QB), -jnp.inf, F32)
+
+    def tile(h, cols, top, other, other_cols):
+        shift = top * turns
+        total = jnp.zeros((1, QB), F32)
+        other_top = lowest
         for c in range(chunks):
+            other_top = score(other, other_cols, c, other_top)
             rows = pl.ds(c * KC, KC)
-            s = dot(k_s[rows, :], qt)
-            s_s[rows, :] = s
-            m = jnp.max(s, axis=0, keepdims=True)
-            top = m if top is None else jnp.maximum(top, m)
-        shift = top * (SCALE * LOG2E)
-        total = jnp.zeros((1, QB), F32)
-        for c in range(chunks):
-            rows = pl.ds(c * KC, KC)
-            e = jnp.exp2(s_s[rows, :] * (SCALE * LOG2E) - shift)
+            e = jnp.exp2(s_s[h, rows, :] * turns - shift)
             p_s[h, rows, cols] = e.astype(BF)
             total = total + jnp.sum(e, axis=0, keepdims=True)
         inv = jnp.broadcast_to(1.0 / total, (8, QB))
@@ -545,114 +564,146 @@
         down = inv.T[:, 0:1]
         dam[h, cols, :] = (dam[h, cols, :].astype(F32) * down).astype(BF)
         qm[h, cols, :] = (qm[h, cols, :].astype(F32) * down).astype(BF)
-        return carry
-
-    lax.fori_loop(0, steps, forward, 0)
-
-    def grads(c, rows, right, scale):
+        return other_top
+
+    def forward(i, top):
+        cols = rows_at(i, QB)
+        after = rows_at(jnp.minimum(i + 1, tiles - 1), QB)
+        top = tile(0, cols, top, 1, cols)
+
+        @pl.when(i == 1)
+        def _():
+            fv.step(3)
+
+        return tile(1, cols, top, 0, after)
+
+    top = lowest
+    for c in range(chunks):
+        top = score(0, pl.ds(0, QB), c, top)
+    lax.fori_loop(0, tiles, forward, top)
+
+    wide = 4 * BLOCK
+
+    def grads(c, right, scale):
+        rows = rows_at(c, wide)
         g = dot(p_s[0, rows, :], right[0]) + dot(p_s[1, rows, :], right[1])
         if scale is not None:
             g = g * scale
         g = g.astype(BF)
-        for b in range(KC // BLOCK):
-            grad_s[c * (KC // BLOCK) + b] = g[b * BLOCK : (b + 1) * BLOCK, :]
+        for b in range(4):
+            grad_s[c * 4 + b] = g[b * BLOCK : (b + 1) * BLOCK, :]
+
+    def hand_out(sent, held, low, high):
+        for e in range(low, high):
+            held[0, e] = grad_s[pack[views + 8, e]]
+            for k in range(1, NY):
+                sent[k - 1, e] = grad_s[pack[views + 8, k * NZ + e]]
 
     def value_grads(c, carry):
-        grads(c, rows_at(c, KC), dam, None)
+        @pl.when(c == 1)
+        def _():
+            hand_out(sent_v, held_v, 7, 8)
+            rv.start_y(0)
+
+        @pl.when(c == 3)
+        def _():
+            hand_out(sent_v, held_v, 5, 7)
+            rv.start_y(1)
+
+        grads(c, dam, None)
         return carry
 
-    def hand_out(sent, held):
-        for e in range(NZ):
-            held[0, e] = grad_s[pack[views + slots, e]]
-        for k in range(1, NY):
-            for e in range(NZ):
-                sent[k - 1, e] = grad_s[pack[views + slots, k * NZ + e]]
-
-    lax.fori_loop(0, chunks, value_grads, 0)
     fv.step(4)
-    hand_out(sent_v, held_v)
-    rv.start_y(0)
+    lax.fori_loop(0, keys // wide, value_grads, 0)
     fv.step(5)
-    rv.start_y(1)
     rv.step(1)
     fv.step(6)
+    hand_out(sent_v, held_v, 0, 5)
     rv.start_y(2)
+    rv.step(2)
+    rv.step(3)
     rv.start_y(3)
     rv.start_y(4)
     for j in range(slots):
+        kt_s[:, pl.ds(j * BLOCK, BLOCK)] = k_s[pl.ds(j * BLOCK, BLOCK), :].T
+    fv.step(7)
+    for j in range(slots):
         rows = pl.ds(j * BLOCK, BLOCK)
-        block = got_v[pack[views + j, 0]]
+        block = got_v[pack[views, j]]
         v_s[rows, :] = block
         vt_s[:, rows] = block.T
 
     def attend(i, carry):
-        h = lax.rem(i, 2)
-        cols = rows_at(i // 2, QB)
-        band = rows_at(h, HEAD_DIM)
-        att = dot(vt_s[band, :], p_s[h, :, cols]) * inv_s[h, 0:1, cols]
-        att = att.astype(BF)
-        att_t[band, cols] = att
-        delta = jnp.sum(
-            att.astype(F32) * datm[h, band, cols].astype(F32), axis=0, keepdims=True
-        )
-        delta_s[h, :, cols] = jnp.broadcast_to(delta, (8, QB))
+        @pl.when(i == 3)
+        def _():
+            rv.step(4)
+
+        cols = rows_at(i, QB)
+        for h in range(2):
+            band = pl.ds(h * HEAD_DIM, HEAD_DIM)
+            att = dot(vt_s[band, :], p_s[h, :, cols]) * inv_s[h, 0:1, cols]
+            att = att.astype(BF)
+            att_t[band, cols] = att
+            delta = jnp.sum(
+                att.astype(F32) * datm[h, band, cols].astype(F32), axis=0, keepdims=True
+            )
+            delta_s[h, :, cols] = jnp.broadcast_to(delta, (8, QB))
         return carry
 
-    lax.fori_loop(0, steps, attend, 0)
+    lax.fori_loop(0, tiles, attend, 0)
     att_s[...] = att_t[...].T
     at.step(0)
+    rv.step(5)
 
     def key_grads(c, carry):
         @pl.when(c == 1)
         def _():
-            rv.step(2)
-            rv.step(3)
-
-        @pl.when(c == 6)
+            hand_out(sent_k, held_k, 7, 8)
+            rk.start_y(0)
+
+        @pl.when(c == 3)
         def _():
-            at.step(1)
-
-        rows = rows_at(c, KC)
-        right = v_s[rows, :]
+            hand_out(sent_k, held_k, 5, 7)
+            rk.start_y(1)
+            rk.step(1)
+            rv.step(6)
+
+        rows = rows_at(c, wide)
         for h in range(2):
-            for i in range(tokens // QB):
+            for i in range(tiles):
                 cols = pl.ds(i * QB, QB)
-                dp = dot(right, datm[h, :, cols]) - delta_s[h, 0:1, cols]
+                dp = dot(v_s[rows, :], datm[h, :, cols]) - delta_s[h, 0:1, cols]
                 p_s[h, rows, cols] = (p_s[h, rows, cols].astype(F32) * dp).astype(BF)
-        grads(c, rows, qm, SCALE)
+        grads(c, qm, SCALE)
         return carry
 
-    lax.fori_loop(0, chunks, key_grads, 0)
-    hand_out(sent_k, held_k)
-    rk.start_y(0)
-    rk.start_y(1)
-    rv.step(4)
+    lax.fori_loop(0, keys // wide, key_grads, 0)
+    hand_out(sent_k, held_k, 0, 5)
     rk.start_y(2)
     rk.start_y(3)
     rk.start_y(4)
-    for j in range(slots):
-        kt_s[:, pl.ds(j * BLOCK, BLOCK)] = k_s[pl.ds(j * BLOCK, BLOCK), :].T
+    at.step(1)
 
     def query_grads(i, carry):
-        @pl.when(i == 4)
+        @pl.when(i == 3)
         def _():
-            rk.step(1)
-
-        h = lax.rem(i, 2)
-        cols = rows_at(i // 2, QB)
-        band = rows_at(h, HEAD_DIM)
-        dq = dot(kt_s[band, :], p_s[h, :, cols]) * (inv_s[h, 0:1, cols] * SCALE)
-        dq_t[band, cols] = dq.astype(BF)
+            rk.step(2)
+
+        cols = rows_at(i, QB)
+        for h in range(2):
+            band = pl.ds(h * HEAD_DIM, HEAD_DIM)
+            dq = dot(kt_s[band, :], p_s[h, :, cols]) * (inv_s[h, 0:1, cols] * SCALE)
+            dq_t[band, cols] = dq.astype(BF)
         return carry
 
-    lax.fori_loop(0, steps, query_grads, 0)
-    rk.step(2)
-    rv.step(5)
+    lax.fori_loop(0, tiles, query_grads, 0)
+    rk.step(3)
+    rv.step(7)
+    dq_ref[...] = dq_t[...].T
+    stores[0].start()
     at.step(2)
-    rk.step(3)
-    rv.step(6)
-    dq_ref[...] = dq_t[...].T
     rk.step(4)
+    rk.step(5)
     loads[5].wait()
     at.step(3)
 
@@ -665,19 +716,25 @@
         mixed_ref[rows, :] = acc.astype(BF)
         return carry
 
-    rk.step(5)
-    rv.step(7)
+    lax.fori_loop(0, tokens // QB, mix, 0)
+    stores[1].start()
+    rk.step(6)
     rv.step(8)
-    rk.step(6)
-    lax.fori_loop(0, tokens // QB, mix, 0)
-    fk.step(7)
-    fv.step(7)
+    rv.step(9)
+    stores[2].start()
+    rk.step(7)
+    fk.step(8)
+    fv.step(8)
     og.step(4)
     at.step(4)
-    rv.step(9)
-    rk.step(7)
+    rv.step(10)
     rk.step(8)
+    stores[3].start()
     rk.step(9)
+    stores[4].start()
+    rk.step(10)
+    for store in stores:
+        store.wait()
 
 
 def layer(sv, sb, q, k, v, w, og):
@@ -699,7 +756,7 @@
         layer_kernel,
         out_shape=(rows, rows, cut, cut),
         in_specs=[vm, vm] + [hbm] * 5,
-        out_specs=(vm,) * 4,
+        out_specs=(hbm,) * 4,
         scratch_shapes=bufs(Fetch) + bufs(Fetch) + bufs(Return) + bufs(Return) + [
             vmem(NB, BLOCK, COLS),
             vmem(NB, BLOCK, COLS),
@@ -723,19 +780,23 @@
             vmem(COLS, keys),
             vmem(keys, COLS),
             vmem(COLS, keys),
-            vmem(keys, QB, dtype=F32),
+            vmem(2, keys, QB, dtype=F32),
             vmem(2, keys, tokens),
             vmem(COLS, tokens),
             vmem(COLS, tokens),
             vmem(slots, BLOCK, COLS),
             vmem(tokens, COLS),
+            vmem(tokens, COLS),
+            vmem(tokens, COLS),
+            vmem(NB, BLOCK, COLS),
+            vmem(NB, BLOCK, COLS),
             vmem(2, 8, tokens, dtype=F32),
             vmem(2, 8, tokens, dtype=F32),
-            vmem(views + slots + 8, BLOCK, dtype=jnp.int32),
-            pltpu.SMEM((views + slots + 8, BLOCK), jnp.int32),
+            vmem(views + 16, BLOCK, dtype=jnp.int32),
+            pltpu.SMEM((views + 16, BLOCK), jnp.int32),
             pltpu.SemaphoreType.DMA((136,)),
             pltpu.SemaphoreType.DMA((136,)),
-            pltpu.SemaphoreType.DMA((8,)),
+            pltpu.SemaphoreType.DMA((12,)),
         ],
         compiler_params=pltpu.CompilerParams(
             collective_id=0, has_side_effects=True, vmem_limit_bytes=56 * 2**20

time: 107 us -> 98.2 us (0.918)
  Pallas kernels: 107 us -> 97.3 us
    pallas_call x1, Pallas kernels: 104 us -> 95.2 us  [layer(): pl.pallas_call(layer_kernel, out_shape=(rows, rows, cut, cut), in_specs=[...]
where the time goes in v5:
time: 98.2 us; the launch traced here: 98 us
  Pallas kernels  97.3 us (99%)
    pallas_call x1, Pallas kernels, layer(): pl.pallas_call(layer_kernel, out_shape=(rows, rows, cut, cut), in_specs=[...  95.2 us
    pallas_call x1, Pallas kernels, finish(): pl.pallas_call(finish_kernel, out_shape=tuple((jax.ShapeDtypeStruct(a.sha...  2.18 us

profile of v5, /device:TPU:2, one launch (start us, length us, event | category | flops | bytes accessed | tf_op | source)
XLA Modules:
  0.0 98.0 jit_solution(6307775620777245581)
XLA Ops:
  0.6 95.2 %layer.1 = (bf16[1024,128]{1,0:T(8,128)(2,1)}, bf16[1024,128]{1,0:T(8,128)(2,1)}, bf16[8,128,128]{2,1,0:T(8,128)(2,1)}, bf16[8,128,128]{2,1,0:T(8,128)(2,1)}) custom-call(s32[16,32]{1,0:T(8,128)} %bitcast.8, s32[16,32]{1,0:T(8,128)} %bitcast.9, bf16[1024,128]{1,0:T(8,128)(2,1)} %q_hbm.1, bf16[8,128,128]{2,1,0:T(8,128)(2,1)} %bitcast.6, ...), custom_call_target="tpu_custom_call" | custom-call | tf_op jit(solution)/shard_map/layer/pallas_call | solution.py:755
  95.8 2.2 %finish.1 = (bf16[1024,128]{1,0:T(8,128)(2,1)}, bf16[1024,128]{1,0:T(8,128)(2,1)}, bf16[8,128,128]{2,1,0:T(8,128)(2,1)}, bf16[8,128,128]{2,1,0:T(8,128)(2,1)}) custom-call(bf16[1024,128]{1,0:T(8,128)(2,1)} %get-tuple-element.12.refs_0_, bf16[1024,128]{1,0:T(8,128)(2,1)} %get-tuple-element.13.refs_1_, bf16[8,128,128]{2,1,0:T(8,128)(2,1)} %get-tuple-element.14.refs_2_, ...), custom_call_target="tpu_custom_call" | custom-call | tf_op jit(solution)/shard_map/finish/pallas_call | solution.py:821

commit v6 on v5

--- a/solution.py
+++ b/solution.py
@@ -26,17 +26,16 @@
 
 
 class Copies:
-    def __init__(self, send, recv):
-        self.send, self.recv, self.n = send, recv, 0
+    def __init__(self, send, recv, sends, recvs):
+        self.send, self.recv = send, recv
+        self.sends, self.recvs = list(sends), list(recvs)
 
     def make(self, src, dst, device):
-        i = self.n
-        self.n += 1
         return pltpu.make_async_remote_copy(
             src_ref=src,
             dst_ref=dst,
-            send_sem=self.send.at[i],
-            recv_sem=self.recv.at[i],
+            send_sem=self.send.at[self.sends.pop(0)],
+            recv_sem=self.recv.at[self.recvs.pop(0)],
             device_id=device,
             device_id_type=MESH,
         )
@@ -436,7 +435,6 @@
         send, recv, local,
     ) = scratch[24:]
     here = Place()
-    copies = Copies(send, recv)
     slots, views = sv_ref.shape
     keys = slots * BLOCK
     tokens = q_s.shape[0]
@@ -475,12 +473,24 @@
     routes(here.view, sv_ref, sb_ref, pack_v)
     tables.start()
 
-    og = Gather(here, copies, og_own, og_all)
-    fk = Fetch(here, copies, pack, k_own, got_k, fbk)
-    fv = Fetch(here, copies, pack, v_own, got_v, fbv)
-    at = Gather(here, copies, att_s, at_all)
-    rk = Return(here, copies, pack, sent_k, held_k, ok_ref, rbk)
-    rv = Return(here, copies, pack, sent_v, held_v, ov_ref, rbv)
+    def span(a, n):
+        return list(range(a, a + n))
+
+    gat = span(58, 8)
+    og = Gather(here, Copies(send, recv, span(62, 8), gat), og_own, og_all)
+    at = Gather(here, Copies(send, recv, span(62, 8), span(66, 8)), att_s, at_all)
+    fk = Fetch(here, Copies(send, recv, span(0, 29), span(0, 29)), pack, k_own, got_k, fbk)
+    fv = Fetch(here, Copies(send, recv, span(31, 29), span(29, 29)), pack, v_own, got_v, fbv)
+    rv = Return(
+        here,
+        Copies(send, recv, span(0, 31), span(0, 14) + gat[0:1] + span(14, 15) + gat[1:2]),
+        pack, sent_v, held_v, ov_ref, rbv,
+    )
+    rk = Return(
+        here,
+        Copies(send, recv, span(31, 31), span(29, 14) + gat[2:3] + span(43, 15) + gat[3:4]),
+        pack, sent_k, held_k, ok_ref, rbk,
+    )
 
     arrived()
     loads[0].wait()
@@ -584,11 +594,9 @@
 
     wide = 4 * BLOCK
 
-    def grads(c, right, scale):
+    def grads(c, right):
         rows = rows_at(c, wide)
         g = dot(p_s[0, rows, :], right[0]) + dot(p_s[1, rows, :], right[1])
-        if scale is not None:
-            g = g * scale
         g = g.astype(BF)
         for b in range(4):
             grad_s[c * 4 + b] = g[b * BLOCK : (b + 1) * BLOCK, :]
@@ -610,10 +618,12 @@
             hand_out(sent_v, held_v, 5, 7)
             rv.start_y(1)
 
-        grads(c, dam, None)
+        grads(c, dam)
         return carry
 
     fv.step(4)
+    fk.step(8)
+    og.step(4)
     lax.fori_loop(0, keys // wide, value_grads, 0)
     fv.step(5)
     rv.step(1)
@@ -651,6 +661,7 @@
         return carry
 
     lax.fori_loop(0, tiles, attend, 0)
+    fv.step(8)
     att_s[...] = att_t[...].T
     at.step(0)
     rv.step(5)
@@ -665,16 +676,25 @@
         def _():
             hand_out(sent_k, held_k, 5, 7)
             rk.start_y(1)
+            rv.step(6)
             rk.step(1)
-            rv.step(6)
 
         rows = rows_at(c, wide)
+        total, held = None, None
         for h in range(2):
             for i in range(tiles):
                 cols = pl.ds(i * QB, QB)
-                dp = dot(v_s[rows, :], datm[h, :, cols]) - delta_s[h, 0:1, cols]
-                p_s[h, rows, cols] = (p_s[h, rows, cols].astype(F32) * dp).astype(BF)
-        grads(c, qm, SCALE)
+                dp = dot(v_s[rows, :], datm[h, :, cols])
+                if held is not None:
+                    part = dot(*held)
+                    total = part if total is None else total + part
+                dp = dp - delta_s[h, 0:1, cols]
+                ds = (p_s[h, rows, cols].astype(F32) * dp).astype(BF)
+                p_s[h, rows, cols] = ds
+                held = (ds, qm[h, cols, :])
+        total = ((total + dot(*held)) * SCALE).astype(BF)
+        for b in range(4):
+            grad_s[c * 4 + b] = total[b * BLOCK : (b + 1) * BLOCK, :]
         return carry
 
     lax.fori_loop(0, keys // wide, key_grads, 0)
@@ -723,9 +743,6 @@
     rv.step(9)
     stores[2].start()
     rk.step(7)
-    fk.step(8)
-    fv.step(8)
-    og.step(4)
     at.step(4)
     rv.step(10)
     rk.step(8)
@@ -794,8 +811,8 @@
             vmem(2, 8, tokens, dtype=F32),
             vmem(views + 16, BLOCK, dtype=jnp.int32),
             pltpu.SMEM((views + 16, BLOCK), jnp.int32),
-            pltpu.SemaphoreType.DMA((136,)),
-            pltpu.SemaphoreType.DMA((136,)),
+            pltpu.SemaphoreType.DMA((70,)),
+            pltpu.SemaphoreType.DMA((74,)),
             pltpu.SemaphoreType.DMA((12,)),
         ],
         compiler_params=pltpu.CompilerParams(

time: 98.2 us -> 95.3 us (0.970)
  Pallas kernels: 97.3 us -> 94 us
    pallas_call x1, Pallas kernels: 95.2 us -> 91.8 us  [layer(): pl.pallas_call(layer_kernel, out_shape=(rows, rows, cut, cut), in_specs=[...]
where the time goes in v6:
time: 95.3 us; the launch traced here: 94.6 us
  Pallas kernels  94 us (99%)
    pallas_call x1, Pallas kernels, layer(): pl.pallas_call(layer_kernel, out_shape=(rows, rows, cut, cut), in_specs=[...  91.8 us
    pallas_call x1, Pallas kernels, finish(): pl.pallas_call(finish_kernel, out_shape=tuple((jax.ShapeDtypeStruct(a.sha...  2.18 us

profile of v6, /device:TPU:2, one launch (start us, length us, event | category | flops | bytes accessed | tf_op | source)
XLA Modules:
  0.0 94.6 jit_solution(16726824761602796530)
XLA Ops:
  0.6 91.8 %layer.1 = (bf16[1024,128]{1,0:T(8,128)(2,1)}, bf16[1024,128]{1,0:T(8,128)(2,1)}, bf16[8,128,128]{2,1,0:T(8,128)(2,1)}, bf16[8,128,128]{2,1,0:T(8,128)(2,1)}) custom-call(s32[16,32]{1,0:T(8,128)} %bitcast.8, s32[16,32]{1,0:T(8,128)} %bitcast.9, bf16[1024,128]{1,0:T(8,128)(2,1)} %q_hbm.1, bf16[8,128,128]{2,1,0:T(8,128)(2,1)} %bitcast.6, ...), custom_call_target="tpu_custom_call" | custom-call | tf_op jit(solution)/shard_map/layer/pallas_call | solution.py:772
  92.4 2.2 %finish.1 = (bf16[1024,128]{1,0:T(8,128)(2,1)}, bf16[1024,128]{1,0:T(8,128)(2,1)}, bf16[8,128,128]{2,1,0:T(8,128)(2,1)}, bf16[8,128,128]{2,1,0:T(8,128)(2,1)}) custom-call(bf16[1024,128]{1,0:T(8,128)(2,1)} %get-tuple-element.12.refs_0_, bf16[1024,128]{1,0:T(8,128)(2,1)} %get-tuple-element.13.refs_1_, bf16[8,128,128]{2,1,0:T(8,128)(2,1)} %get-tuple-element.14.refs_2_, ...), custom_call_target="tpu_custom_call" | custom-call | tf_op jit(solution)/shard_map/finish/pallas_call | solution.py:838

commit v7 on v6

--- a/solution.py
+++ b/solution.py
@@ -287,8 +287,11 @@
             for i in range(2):
                 k = lax.rem(2 * s + i + NY - here.y, NY)
                 self.c4.append(mk(held.at[k, 7], four.at[s, i], way))
-        for s, way in enumerate(ways):
-            self.c3.append(mk(held.at[:, 5 + s], three.at[s, pl.ds(0, 4)], way))
+        for k, size in ((0, 1), (1, 3)):
+            for s, way in enumerate(ways):
+                self.c3.append(
+                    mk(held.at[pl.ds(k, size), 5 + s], three.at[s, pl.ds(k, size)], way)
+                )
         for s, way in enumerate(ways):
             self.c3.append(mk(four.at[s], three.at[s, pl.ds(4, 2)], way))
         for part in range(2):
@@ -330,18 +333,21 @@
     def step(self, n):
         here, table = self.here, self.table
         h = NB // 2
+        if n == 0:
+            for copy in self.c3[:2]:
+                copy.start()
         if n == 1:
             self.wait_y(0)
             for copy in self.c4:
                 copy.start()
         if n == 2:
             self.wait_y(1)
-            for copy in self.c3[:2]:
+            for copy in self.c3[2:4]:
                 copy.start()
         if n == 3:
             for copy in self.c4:
                 copy.wait_recv()
-            for copy in self.c3[2:]:
+            for copy in self.c3[4:]:
                 copy.start()
         if n in (4, 5):
             part = n - 4
@@ -477,18 +483,18 @@
         return list(range(a, a + n))
 
     gat = span(58, 8)
-    og = Gather(here, Copies(send, recv, span(62, 8), gat), og_own, og_all)
-    at = Gather(here, Copies(send, recv, span(62, 8), span(66, 8)), att_s, at_all)
+    og = Gather(here, Copies(send, recv, span(66, 8), gat), og_own, og_all)
+    at = Gather(here, Copies(send, recv, span(66, 8), span(66, 8)), att_s, at_all)
     fk = Fetch(here, Copies(send, recv, span(0, 29), span(0, 29)), pack, k_own, got_k, fbk)
-    fv = Fetch(here, Copies(send, recv, span(31, 29), span(29, 29)), pack, v_own, got_v, fbv)
+    fv = Fetch(here, Copies(send, recv, span(33, 29), span(29, 29)), pack, v_own, got_v, fbv)
     rv = Return(
         here,
-        Copies(send, recv, span(0, 31), span(0, 14) + gat[0:1] + span(14, 15) + gat[1:2]),
+        Copies(send, recv, span(0, 33), span(0, 14) + gat[0:1] + span(14, 15) + gat[1:4]),
         pack, sent_v, held_v, ov_ref, rbv,
     )
     rk = Return(
         here,
-        Copies(send, recv, span(31, 31), span(29, 14) + gat[2:3] + span(43, 15) + gat[3:4]),
+        Copies(send, recv, span(33, 33), span(29, 14) + gat[4:5] + span(43, 15) + gat[5:8]),
         pack, sent_k, held_k, ok_ref, rbk,
     )
 
@@ -617,6 +623,7 @@
         def _():
             hand_out(sent_v, held_v, 5, 7)
             rv.start_y(1)
+            rv.step(0)
 
         grads(c, dam)
         return carry
@@ -644,9 +651,13 @@
         vt_s[:, rows] = block.T
 
     def attend(i, carry):
-        @pl.when(i == 3)
+        @pl.when(i == 1)
         def _():
             rv.step(4)
+
+        @pl.when(i == 2)
+        def _():
+            rv.step(5)
 
         cols = rows_at(i, QB)
         for h in range(2):
@@ -664,7 +675,6 @@
     fv.step(8)
     att_s[...] = att_t[...].T
     at.step(0)
-    rv.step(5)
 
     def key_grads(c, carry):
         @pl.when(c == 1)
@@ -677,6 +687,7 @@
             hand_out(sent_k, held_k, 5, 7)
             rk.start_y(1)
             rv.step(6)
+            rk.step(0)
             rk.step(1)
 
         rows = rows_at(c, wide)
@@ -811,7 +822,7 @@
             vmem(2, 8, tokens, dtype=F32),
             vmem(views + 16, BLOCK, dtype=jnp.int32),
             pltpu.SMEM((views + 16, BLOCK), jnp.int32),
-            pltpu.SemaphoreType.DMA((70,)),
+            pltpu.SemaphoreType.DMA((74,)),
             pltpu.SemaphoreType.DMA((74,)),
             pltpu.SemaphoreType.DMA((12,)),
         ],

time: 95.3 us -> 95.8 us (level)
  no operation moved by 1% of the time
where the time goes in v7:
time: 95.8 us; the launch traced here: 95 us
  Pallas kernels  94.3 us (98%)
    pallas_call x1, Pallas kernels, layer(): pl.pallas_call(layer_kernel, out_shape=(rows, rows, cut, cut), in_specs=[...  92.1 us
    pallas_call x1, Pallas kernels, finish(): pl.pallas_call(finish_kernel, out_shape=tuple((jax.ShapeDtypeStruct(a.sha...  2.18 us

profile of v7, /device:TPU:2, one launch (start us, length us, event | category | flops | bytes accessed | tf_op | source)
XLA Modules:
  0.0 95.0 jit_solution(4884518461914667035)
XLA Ops:
  0.6 92.1 %layer.1 = (bf16[1024,128]{1,0:T(8,128)(2,1)}, bf16[1024,128]{1,0:T(8,128)(2,1)}, bf16[8,128,128]{2,1,0:T(8,128)(2,1)}, bf16[8,128,128]{2,1,0:T(8,128)(2,1)}) custom-call(s32[16,32]{1,0:T(8,128)} %bitcast.8, s32[16,32]{1,0:T(8,128)} %bitcast.9, bf16[1024,128]{1,0:T(8,128)(2,1)} %q_hbm.1, bf16[8,128,128]{2,1,0:T(8,128)(2,1)} %bitcast.6, ...), custom_call_target="tpu_custom_call" | custom-call | tf_op jit(solution)/shard_map/layer/pallas_call | solution.py:783
  92.8 2.2 %finish.1 = (bf16[1024,128]{1,0:T(8,128)(2,1)}, bf16[1024,128]{1,0:T(8,128)(2,1)}, bf16[8,128,128]{2,1,0:T(8,128)(2,1)}, bf16[8,128,128]{2,1,0:T(8,128)(2,1)}) custom-call(bf16[1024,128]{1,0:T(8,128)(2,1)} %get-tuple-element.12.refs_0_, bf16[1024,128]{1,0:T(8,128)(2,1)} %get-tuple-element.13.refs_1_, bf16[8,128,128]{2,1,0:T(8,128)(2,1)} %get-tuple-element.14.refs_2_, ...), custom_call_target="tpu_custom_call" | custom-call | tf_op jit(solution)/shard_map/finish/pallas_call | solution.py:849
